TPU v7x, 128 devices: a whole 4x4x4 slice. The times are simulated.
128 devices in a mesh: seq: 16 (over x, y), section: 8 (over z, core).
Axes of the slice: x: 4, y: 4, z: 4, core: 2. Of those that a mesh axis runs over, the one named last changes fastest.
Arguments:
- queries: bfloat16 [2048, 4096], P('seq', 'section'), may hold values from -10 to 10
- keys: bfloat16 [2048, 1024], P('seq', 'section'), may hold values from -10 to 10
- values: bfloat16 [2048, 1024], P('seq', 'section'), may hold values from -18 to 18
- residual: bfloat16 [2048, 8192], P(None, 'seq'), may hold values from -8 to 8
- out_weight: bfloat16 [4096, 8192], P('section', 'seq'), may hold values from -0.09375 to 0.09375
- norm_gain: float32 [8192], P('seq'), may hold values from 0.1 to 1.9
- in_weight: bfloat16 [8192, 2, 16, 512], P('seq', None, None, 'section'), may hold values from -0.09375 to 0.09375
- conv_weight: float32 [8192, 4], P(('seq', 'section')), may hold values from -3 to 3
- conv_bias: float32 [8192], P(('seq', 'section')), may hold values from -0.5 to 0.5
- proj_weight: bfloat16 [8192, 272], P(('seq', 'section')), may hold values from -0.0625 to 0.0625
- dt_weight: bfloat16 [256, 8192], P(None, ('seq', 'section')), may hold values from -0.375 to 0.375
- dt_bias: float32 [8192], P(('seq', 'section')), may hold values from -3 to 0
- a_log: float32 [8192, 8], P(('seq', 'section')), may hold values from -7 to 0
- skip_gain: float32 [8192], P(('seq', 'section')), may hold values from -2.5 to 2.5
Outputs:
- mixer_out: bfloat16 [8192, 2048], P(('seq', 'section'))
All inputs are finite; a program needn't handle non-finite values.
Results may differ from a plain program's by a relative error of at most 0.03.
Values may be sent and summed in bfloat16 or wider, within the bound.
A program may use at most 128 MiB of HBM per device.

v0:
```python
import math

import jax
import jax.numpy as jnp
from jax import lax
from jax.sharding import PartitionSpec as P

D = 8192
HD = 128
GROUP = 4
NST = 8
DT_RANK = 256
CONV = 4
SCAN_BLOCK = 128


norm_eps = 1e-05


def fold_half(carried, query_part, query_first, key_part, value_part, first_row):
    half_rows = query_part.shape[0]
    key_count = key_part.shape[0]
    heads_kv = key_part.shape[1] // HD
    key_heads = key_part.reshape(key_count, heads_kv, HD)
    value_heads = value_part.reshape(key_count, heads_kv, HD)
    query_pos = query_first + jnp.arange(half_rows, dtype=jnp.int32)
    key_pos = jnp.arange(key_count, dtype=jnp.int32)

    def update(previous):
        running_max, weight_sum, accumulated = previous
        scores = jnp.einsum(
            "qhgd,khd->hgqk", query_part, key_heads, preferred_element_type=jnp.float32
        ) / math.sqrt(HD)
        allowed = query_pos[:, None] >= key_pos[None, :]
        scores = jnp.where(allowed, scores, -1e30)
        new_max = jnp.maximum(running_max, jnp.max(scores, axis=3))
        exponent_terms = jnp.where(allowed, jnp.exp(scores - new_max[..., None]), 0.0)
        weight_sum = jnp.sum(exponent_terms, axis=3)
        weights_bf = exponent_terms.astype(jnp.bfloat16)
        moved = jnp.einsum(
            "hgqk,khd->qhgd", weights_bf, value_heads, preferred_element_type=jnp.float32
        )
        accumulated = moved
        return (new_max, weight_sum, accumulated)

    def unchanged(previous):
        return previous

    return lax.cond(first_row <= query_first + half_rows - 1, update, unchanged, carried)


def finish_half(carried):
    running_max, weight_sum, accumulated = carried
    result = accumulated / jnp.transpose(weight_sum, (2, 0, 1))[..., None]
    return result.astype(jnp.bfloat16).reshape(result.shape[0], -1)


def body(
    queries,
    keys,
    values,
    residual,
    out_weight,
    norm_gain,
    in_weight,
    conv_weight,
    conv_bias,
    proj_weight,
    dt_weight,
    dt_bias,
    a_log,
    skip_gain,
):
    tok_rows = queries.shape[0]
    half_rows = tok_rows // 2
    heads_kv = keys.shape[1] // HD
    seq_rank = lax.axis_index("seq")
    query_halves = queries.reshape(2, half_rows, heads_kv, GROUP, HD)
    first_half = query_halves[0]
    second_half = query_halves[1]
    first_first = seq_rank * tok_rows
    second_first = seq_rank * tok_rows + half_rows
    start_state = (
        jnp.full((heads_kv, GROUP, half_rows), -1e30, jnp.float32),
        jnp.zeros((heads_kv, GROUP, half_rows), jnp.float32),
        jnp.zeros((half_rows, heads_kv, GROUP, HD), jnp.float32),
    )
    carried = (start_state, start_state)
    first_row = jnp.int32(0)
    key_part = lax.all_gather(keys, "seq", axis=0, tiled=True)
    value_part = lax.all_gather(values, "seq", axis=0, tiled=True)
    first_out = finish_half(
        fold_half(carried[0], first_half, first_first, key_part, value_part, first_row)
    )
    second_out = finish_half(
        fold_half(carried[1], second_half, second_first, key_part, value_part, first_row)
    )
    attended = jnp.concatenate([first_out, second_out], axis=0)
    branch_part = jnp.dot(
        lax.all_gather(attended, "seq", axis=0, tiled=True),
        out_weight,
        preferred_element_type=jnp.float32,
    )
    branch_total = lax.psum(branch_part.astype(jnp.bfloat16), "section").astype(jnp.float32)
    hidden = residual.astype(jnp.float32) + branch_total
    squares = lax.psum(jnp.sum(hidden * hidden, axis=1), "seq")
    inv_rms = lax.rsqrt(squares / D + norm_eps)
    normed = (hidden * inv_rms[:, None] * norm_gain[None, :]).astype(jnp.bfloat16)
    seq_len = normed.shape[0]
    channels = conv_weight.shape[0]
    mixed_in = lax.psum_scatter(
        jnp.einsum("ld,dksc->skcl", normed, in_weight, preferred_element_type=jnp.float32).astype(
            jnp.bfloat16
        ),
        "seq",
        scatter_dimension=0,
        tiled=True,
    ).astype(jnp.float32)[0]
    x_path = mixed_in[0]
    z_gate = mixed_in[1]
    padded = jnp.pad(x_path, ((0, 0), (CONV - 1, 0)))
    conv_out = conv_bias[:, None] + jnp.zeros((channels, seq_len), jnp.float32)
    for offset in range(CONV):
        conv_out = (
            conv_out + conv_weight[:, offset : offset + 1] * padded[:, offset : offset + seq_len]
        )
    inputs = jax.nn.silu(conv_out).astype(jnp.bfloat16)
    local_proj = jnp.einsum("cr,cl->rl", proj_weight, inputs, preferred_element_type=jnp.float32)
    projected = lax.psum(local_proj, ("seq", "section"))
    low_rank = projected[:DT_RANK].astype(jnp.bfloat16)
    in_map = projected[DT_RANK : DT_RANK + NST]
    out_map = projected[DT_RANK + NST :]
    step_size = jax.nn.softplus(
        jnp.einsum("rc,rl->cl", dt_weight, low_rank, preferred_element_type=jnp.float32)
        + dt_bias[:, None]
    )
    decay = -jnp.exp(a_log)
    inputs_float = inputs.astype(jnp.float32)
    block_total = seq_len // SCAN_BLOCK

    def split_blocks(matrix):
        return jnp.moveaxis(matrix.reshape(matrix.shape[0], block_total, SCAN_BLOCK), 1, 0)

    def combine(earlier, later):
        return (earlier[0] * later[0], earlier[1] * later[0] + later[1])

    def scan_block(carried, block_inputs):
        step_block, input_block, in_block, out_block = block_inputs
        factor = jnp.exp(step_block[:, None, :] * decay[:, :, None])
        source = (step_block * input_block)[:, None, :] * in_block[None, :, :]
        cum_factor, cum_source = lax.associative_scan(combine, (factor, source), axis=2)
        states = cum_factor * carried[:, :, None] + cum_source
        readout = jnp.sum(states * out_block[None, :, :], axis=1)
        return (states[:, :, -1], readout)

    block_inputs = (
        split_blocks(step_size),
        split_blocks(inputs_float),
        split_blocks(in_map),
        split_blocks(out_map),
    )
    final_state, readouts = lax.scan(
        scan_block, jnp.zeros((channels, NST), jnp.float32), block_inputs
    )
    readout = jnp.moveaxis(readouts, 0, 1).reshape(channels, seq_len)
    return ((readout + skip_gain[:, None] * inputs_float) * jax.nn.silu(z_gate)).astype(
        jnp.bfloat16
    )


def solution(mesh):
    return jax.shard_map(
        body,
        mesh=mesh,
        in_specs=(
            P("seq", "section"),
            P("seq", "section"),
            P("seq", "section"),
            P(None, "seq"),
            P("section", "seq"),
            P("seq"),
            P("seq", None, None, "section"),
            P(("seq", "section"), None),
            P(("seq", "section")),
            P(("seq", "section"), None),
            P(None, ("seq", "section")),
            P(("seq", "section")),
            P(("seq", "section"), None),
            P(("seq", "section")),
        ),
        out_specs=P(("seq", "section"), None),
        check_vma=False,
    )
```

profile of v0, /device:TPU:1, one launch (start us, length us, event | category | flops | bytes accessed | tf_op | source)
XLA Modules:
  0.0 668.1 jit_solution(6703559895228278824)
XLA Ops:
  6.5 20.1 %all_gather.9 = bf16[2048,128]{1,0:T(8,128)(2,1)S(1)} all-gather(bf16[128,128]{1,0:T(8,128)(2,1)} %param.21), channel_id=1, replica_groups=mesh['seq'=16,'section'=8] {'seq'}, dimensions={0}, use_global_device_ids=true | all-gather | bytes 557056 | tf_op jit(solution)/shard_map/all_gather | solution.py:90
  26.6 17.5 %all_gather.10 = bf16[2048,128]{1,0:T(8,128)(2,1)S(1)} all-gather(bf16[128,128]{1,0:T(8,128)(2,1)} %param.22), channel_id=1, replica_groups=mesh['seq'=16,'section'=8] {'seq'}, dimensions={0}, use_global_device_ids=true | all-gather | bytes 557056 | tf_op jit(solution)/shard_map/all_gather | solution.py:91
  44.1 2.7 conditional.2
  44.3 1.4 fusion.49
  47.0 2.7 conditional.3
  47.1 1.4 fusion.50
  50.6 54.1 %all-gather.2.cloned.1.call-done = bf16[2048,512]{1,0:T(8,128)(2,1)} async-done(((bf16[128,512]{1,0:T(8,128)(2,1)}), bf16[2048,512]{1,0:T(8,128)(2,1)}) %all-gather.2.cloned.1.call-update) | async-done | bytes 2097168 | tf_op jit(solution)/shard_map/all_gather | solution.py:100
  104.7 4.3 convolution_convert_fusion
  109.0 65.2 %all-reduce.34.cloned.1.call-done = bf16[2048,512]{1,0:T(8,128)(2,1)} async-done(((bf16[2048,512]{1,0:T(8,128)(2,1)}), bf16[2048,512]{1,0:T(8,128)(2,1)}) %all-reduce.34.cloned.1.call-update) | async-done | bytes 2097168 | tf_op jit(solution)/shard_map/psum | solution.py:104
  174.2 3.0 multiply_reduce_fusion.1
  177.2 33.6 %psum.22 = f32[2048]{0:T(1024)S(1)} all-reduce(f32[2048]{0:T(1024)S(1)} %multiply_reduce_fusion.1), channel_id=1, replica_groups=mesh['seq'=16,'section'=8] {'seq'}, use_global_device_ids=true, to_apply=%region_10.11 | all-reduce | flops 2048 | bytes 16384 | tf_op jit(solution)/shard_map/psum | solution.py:106
  210.9 6.6 fusion.39
  217.5 4.0 convert_bitcast_fusion
  222.7 142.5 %all-reduce.38.cloned.1.call-done = bf16[16,2,64,2048]{3,2,0,1:T(8,128)(2,1)} async-done(((bf16[16,2,64,2048]{3,2,0,1:T(8,128)(2,1)}), bf16[16,2,64,2048]{3,2,0,1:T(8,128)(2,1)}) %all-reduce.38.cloned.1.call-update) | async-done | bytes 8388624
  365.2 3.0 dynamic-slice_convert_fusion
  368.3 1.2 convert_bitcast_fusion.1
  369.5 2.8 convolution_bitcast_fusion.2
  372.4 0.9 copy.109
  373.3 150.7 %all-reduce.36.cloned.1.call-done = f32[272,2048]{1,0:T(8,128)} async-done(((f32[272,2048]{1,0:T(8,128)}), f32[272,2048]{1,0:T(8,128)}) %all-reduce.36.cloned.1.call-update) | async-done | bytes 2228240 | tf_op jit(solution)/shard_map/psum | solution.py:129
  524.0 2.1 fusion.45
  526.1 0.9 copy.110
  526.9 0.9 slice_bitcast_fusion.5
  527.8 130.0 %while.12 = (s32[]{:T(128)}, f32[64,8]{0,1:T(8,128)S(1)}, f32[16,64,128]{1,2,0:T(8,128)}, f32[16,64,128]{2,1,0:T(8,128)}, f32[64,8]{0,1:T(8,128)S(1)}, /*index=5...) while((s32[]{:T(128)}, f32[64,8]{0,1:T(8,128)S(1)}, ...), condition=%wide.region_15.16_spmd, body=%wide.region_13.15_spmd.sunk | while | flops 1284610 | bytes 11625169 | solution.py:162
  527.9 0.8 bitcast_multiply_fusion.2
  544.1 0.8 bitcast_multiply_fusion.2
  552.2 0.8 bitcast_multiply_fusion.2
  560.3 0.8 bitcast_multiply_fusion.2
  568.5 0.8 bitcast_multiply_fusion.2
  576.6 0.8 bitcast_multiply_fusion.2
  592.8 0.8 bitcast_multiply_fusion.2
  657.8 1.7 copy.83
  659.5 2.0 fusion.44
  (1376 shorter events, 120.1 us)
Async XLA Ops:
  6.5 204.3 %copy-start = (bf16[512,2,16,64]{0,3,2,1:T(8,128)(2,1)S(1)}, bf16[512,2,16,64]{0,3,2,1:T(8,128)(2,1)}, u32[]{:S(2)}) copy-start(bf16[512,2,16,64]{0,3,2,1:T(8,128)(2,1)} %param.26) | copy-start | bytes 6291460
  6.5 98.2 %all-gather.2.cloned.1.call-start = ((), (), s32[]{:S(2)}) async-start(), calls=%async_computation | async-start | bytes 2228224 | tf_op jit(solution)/shard_map/all_gather | solution.py:100
  50.6 123.7 %all-reduce.34.cloned.1.call-start = ((), (), s32[]{:S(2)}) async-start(), calls=%async_computation.1 | async-start | bytes 4194304 | tf_op jit(solution)/shard_map/psum | solution.py:104
  109.0 101.9 %copy-start.9 = (f32[512]{0:T(512)S(1)}, f32[512]{0:T(512)}, u32[]{:S(2)}) copy-start(f32[512]{0:T(512)} %param.25) | copy-start | bytes 6148
  109.0 256.2 %all-reduce.38.cloned.1.call-start = ((), (), s32[]{:S(2)}) async-start(), calls=%async_computation.3 | async-start | bytes 16777216
  221.4 0.7 copy-start.10
  221.4 1.2 copy-start.5
  221.5 146.8 %copy-start.6 = (f32[64]{0:T(128)S(1)}, f32[64]{0:T(128)}, u32[]{:S(2)}) copy-start(f32[64]{0:T(128)} %param.28) | copy-start | bytes 772
  221.5 302.5 %all-reduce.36.cloned.1.call-start = ((), (), s32[]{:S(2)}) async-start(), calls=%async_computation.2 | async-start | bytes 4456448 | tf_op jit(solution)/shard_map/psum | solution.py:129
  365.2 4.3 copy-start.2
  369.5 2.9 copy-start.4
  372.4 151.6 %copy-start.3 = (bf16[256,64]{0,1:T(8,128)(2,1)S(1)}, bf16[256,64]{0,1:T(8,128)(2,1)}, u32[]{:S(2)}) copy-start(bf16[256,64]{0,1:T(8,128)(2,1)} %param.30) | copy-start | bytes 98308
  372.4 151.6 %copy-start.7 = (f32[64]{0:T(128)S(1)}, f32[64]{0:T(128)}, u32[]{:S(2)}) copy-start(f32[64]{0:T(128)} %param.31) | copy-start | bytes 772
  527.8 131.7 %copy-start.8 = (f32[64]{0:T(128)S(1)}, f32[64]{0:T(128)}, u32[]{:S(2)}) copy-start(f32[64]{0:T(128)} %param.33) | copy-start | bytes 772
  657.8 3.7 copy-start.1
Sparse Core Ops, SparseCore 0:
  50.7 53.9 all-gather.1
  109.1 65.0 all-reduce.33
  221.6 143.5 all-reduce.37
  372.5 151.4 all-reduce.35
where the time goes:
time: 671 us; the launch traced here: 668 us
  waiting for transfers between devices  413 us (62%)
  local copies, waits for them, and re-layouts  95.4 us (14%)
  blocking collectives  71.1 us (11%)
  other arithmetic  46.1 us (7%)
  matrix products  19.7 us (3%)
  between operations  13.3 us (2%)
  loops' own time  9.46 us (1%)
    psum x1, waiting for transfers between devices, body(): projected = lax.psum(local_proj, ('seq', 'section'))  151 us
    unnamed x5, waiting for transfers between devices  143 us
    psum x1, waiting for transfers between devices, body(): lax.psum(branch_part.astype(jnp.bfloat16), 'section').astype(jnp.float32)  65.2 us
    pad x384, local copies, waits for them, and re-layouts, scan_block(): lax.associative_scan(combine, (factor, source), axis=2)  60.6 us
    all_gather x1, waiting for transfers between devices, body(): lax.all_gather(attended, 'seq', axis=0, tiled=True)  54.1 us
    psum x1, blocking collectives, body(): squares = lax.psum(jnp.sum(hidden * hidden, axis=1), 'seq')  33.6 us
    all_gather x1, blocking collectives, body(): key_part = lax.all_gather(keys, 'seq', axis=0, tiled=True)  20.1 us
    all_gather x1, blocking collectives, body(): value_part = lax.all_gather(values, 'seq', axis=0, tiled=True)  17.5 us
  transfers between devices with their start and end apart: 4, of which 4 were waited for; matrix products, arithmetic and copies ran while one was open for 0% of the time, Pallas kernels for 0%

commit v1 on v0

v1 whole, which is shorter than its diff:
```python
import math

import jax
import jax.numpy as jnp
from jax import lax
from jax.experimental import pallas as pl
from jax.experimental.pallas import tpu as pltpu
from jax.sharding import PartitionSpec as P

D = 8192
HD = 128
GROUP = 4
NST = 8
DT_RANK = 256
CONV = 4
NORM_EPS = 1e-05
MESH = pl.DeviceIdType.MESH
BF = jnp.bfloat16
F32 = jnp.float32
ROWS = 272
SPLIT = 144
LOG2E = math.log2(math.e)
NT = (((1,), (1,)), ((), ()))
TN = (((0,), (0,)), ((), ()))


def nt_dot(a, b, **kw):
    return lax.dot_general(a, b, NT, preferred_element_type=F32, **kw)


def mm(a, b):
    return jnp.dot(a, b, preferred_element_type=F32)


class Comm:
    def __init__(self, send_sem, recv_sem):
        self.send_sem = send_sem
        self.recv_sem = recv_sem
        self.copies = []

    def send(self, src, dst, dev):
        at = len(self.copies)
        copy = pltpu.make_async_remote_copy(
            src_ref=src,
            dst_ref=dst,
            send_sem=self.send_sem.at[at],
            recv_sem=self.recv_sem.at[at],
            device_id=dev,
            device_id_type=MESH,
        )
        copy.start()
        self.copies.append(copy)
        return copy

    def finish(self):
        for copy in self.copies:
            copy.wait_send()


def run(*streams):
    live = list(streams)
    while live:
        for stream in list(live):
            try:
                next(stream)
            except StopIteration:
                live.remove(stream)


def gather_plane(comm, place, size, first, second):
    half = size // 2
    one = comm.send(place(0, 0, 0, size), place(0, 0, 0, size), first[0])
    two = comm.send(place(0, 0, 0, size), place(0, 0, 0, size), first[1])

    def along(df):
        block = place(df, 0, 0, size)
        return comm.send(block, block, second[0]), comm.send(block, block, second[1])

    sent = [(0, along(0))]
    yield
    one.wait_recv()
    block = place(-1, 0, 0, half)
    three = comm.send(block, block, first[0])
    two.wait_recv()
    block = place(1, 0, half, size - half)
    four = comm.send(block, block, first[1])
    sent.append((-1, along(-1)))
    sent.append((1, along(1)))
    yield
    three.wait_recv()
    four.wait_recv()
    sent.append((2, along(2)))
    yield
    last = []
    for df, (up, down) in sent:
        up.wait_recv()
        block = place(df, -1, 0, half)
        last.append(comm.send(block, block, second[0]))
        down.wait_recv()
        block = place(df, 1, half, size - half)
        last.append(comm.send(block, block, second[1]))
    yield
    for copy in last:
        copy.wait_recv()


def ring_gather(comm, place, size, cut, ends, also=None):
    whole = place(0, 0, size)
    up = comm.send(whole, whole, ends[0])
    down = comm.send(whole, whole, ends[1])
    if also:
        also(0)
    yield
    up.wait_recv()
    block = place(-1, 0, cut)
    far_up = comm.send(block, block, ends[0])
    if also:
        also(-1)
    down.wait_recv()
    block = place(1, cut, size - cut)
    far_down = comm.send(block, block, ends[1])
    if also:
        also(1)
    yield
    far_up.wait_recv()
    far_down.wait_recv()
    if also:
        also(2)


def front_kernel(
    q_ref, k_ref, v_ref, res_ref, ow_ref, gain_ref, w_ref, cw_ref, cb_ref, pw_ref,
    uz_ref, g_ref,
    kv, att, cs, cr, zs, zn, zf, act, hid, ssq_out, ssq_in, res, wv,
    s1, r1, s2, r2, own, t1, u1, t2, u2, mixed,
    gs, gr, gz, gzn, gzf, gx, gfull,
    send_sem, recv_sem, local_sem,
):
    s = lax.axis_index("seq")
    c = lax.axis_index("section")
    x, y = s // 4, s % 4
    z, k = c // 2, c % 2
    o = 1 - k

    def seq_of(cx, cy):
        return {"seq": cx * 4 + cy}

    def section_of(cz, ck):
        return {"section": cz * 2 + ck}

    xe = (seq_of((x + 1) % 4, y), seq_of((x + 3) % 4, y))
    ye = (seq_of(x, (y + 1) % 4), seq_of(x, (y + 3) % 4))
    ze = (section_of((z + 1) % 4, k), section_of((z + 3) % 4, k))
    sib = section_of(z, o)

    res_copy = pltpu.make_async_copy(
        res_ref.at[pl.ds(1024 * k + 256 * z, 256)], res, local_sem.at[0]
    )
    res_copy.start()
    w_copy = pltpu.make_async_copy(w_ref, wv, local_sem.at[1])
    w_copy.start()

    barrier = pltpu.get_barrier_semaphore()
    for off in range(1, 16):
        pl.semaphore_signal(
            barrier, inc=1, device_id={"seq": (s + off) % 16}, device_id_type=MESH
        )
    for dev in (*ze, sib):
        pl.semaphore_signal(barrier, inc=1, device_id=dev, device_id_type=MESH)
    kv[x, y, :, 0:HD] = k_ref[...]
    kv[x, y, :, HD:] = v_ref[...]
    pl.semaphore_wait(barrier, 18)

    comm = Comm(send_sem, recv_sem)

    def plane_place(buf, x_first, base, by_rows=True):
        def place(df, ds, start, count):
            if x_first:
                cx, cy = (x + df) % 4, (y + ds) % 4
            else:
                cx, cy = (x + ds) % 4, (y + df) % 4
            return buf.at[cx, cy, pl.ds(base + start, count)]

        return place

    run(
        gather_plane(comm, plane_place(kv, True, 0), 64, xe, ye),
        gather_plane(comm, plane_place(kv, False, 64), 64, ye, xe),
    )

    query_pos = s * 128 + lax.broadcasted_iota(jnp.int32, (128, 2048), 0)
    key_pos = lax.broadcasted_iota(jnp.int32, (128, 2048), 1)
    allowed = query_pos >= key_pos
    key_rows = kv[:, :, :, 0:HD].reshape(2048, HD)
    value_rows = kv[:, :, :, HD:].reshape(2048, HD)
    for g in range(GROUP):
        scores = nt_dot(q_ref[:, g * HD : (g + 1) * HD], key_rows)
        scores = jnp.where(allowed, scores, -1e30)
        top = jnp.max(scores, axis=1, keepdims=True)
        terms = jnp.exp2((scores - top) * (LOG2E / math.sqrt(HD)))
        total = jnp.sum(terms, axis=1, keepdims=True)
        moved = mm(terms.astype(BF), value_rows)
        att[x, y, :, g * HD : (g + 1) * HD] = (moved / total).astype(BF)

    run(
        gather_plane(comm, plane_place(att, True, 0), 64, xe, ye),
        gather_plane(comm, plane_place(att, False, 64), 64, ye, xe),
    )

    def branch(kk, zt):
        rows = att[2 * kk + zt // 2, pl.ds((zt % 2) * 2, 2)].reshape(256, 512)
        return mm(rows, ow_ref[...])

    offsets = (2, 1, 3, 0)
    crossing = []
    for off in offsets:
        zt = (z + off) % 4
        cs[zt] = branch(o, zt).astype(BF)
        crossing.append(comm.send(cs.at[zt], cr.at[zt], sib))
    w_copy.wait()
    res_copy.wait()
    near = []
    for at, off in enumerate(offsets):
        zt = (z + off) % 4
        part = branch(k, zt)
        crossing[at].wait_recv()
        part = part + cr[zt].astype(F32)
        if off == 2:
            zs[0] = part.astype(BF)
            far = (
                comm.send(zs.at[0, 0:128], zf.at[0], ze[0]),
                comm.send(zs.at[0, 128:256], zf.at[1], ze[1]),
            )
        elif off == 1:
            far[0].wait_recv()
            zs[1, 0:128] = (part[0:128] + zf[0].astype(F32)).astype(BF)
            zs[1, 128:256] = part[128:256].astype(BF)
            near.append(comm.send(zs.at[1], zn.at[0], ze[0]))
        elif off == 3:
            far[1].wait_recv()
            zs[2, 0:128] = part[0:128].astype(BF)
            zs[2, 128:256] = (part[128:256] + zf[1].astype(F32)).astype(BF)
            near.append(comm.send(zs.at[2], zn.at[1], ze[1]))
        else:
            part = part + res[...].astype(F32)
            near[0].wait_recv()
            part = part + zn[0].astype(F32)
            near[1].wait_recv()
            hid[...] = part + zn[1].astype(F32)

    hidden = hid[...]
    ssq_out[...] = nt_dot(jnp.ones((8, 512), F32), hidden * hidden, precision=lax.Precision.HIGHEST)
    ssq_in[s] = ssq_out[...]
    squares = [
        comm.send(ssq_out, ssq_in.at[s], {"seq": (s + off) % 16}) for off in range(1, 16)
    ]
    for copy in squares:
        copy.wait_recv()
    total = ssq_in[0]
    for at in range(1, 16):
        total = total + ssq_in[at]
    inv = jnp.transpose(lax.rsqrt(total / D + NORM_EPS))[:, 0:1]
    act[k, z] = (hidden * inv * gain_ref[...]).astype(BF)

    across = []

    def act_place(d, start, count):
        return act.at[k, (z + d) % 4, pl.ds(start, count)]

    def act_also(d):
        block = act.at[k, (z + d) % 4]
        across.append(comm.send(block, block, sib))

    run(ring_gather(comm, act_place, 256, 128, ze, act_also))
    for copy in across:
        copy.wait_recv()

    def rs_half(h, main, main_ends, side, side_ends):
        def weights(p):
            rows = []
            for j in range(4):
                b = (j * 4 + p) if h == 0 else (p * 4 + j)
                rows += [wv[0, b], wv[1, b]]
            return jnp.concatenate(rows, axis=0)

        def product(p, put):
            wide = weights(p)
            for r in range(4):
                acc = nt_dot(act[h, r], wide)
                for j in range(4):
                    put(j, r * 256, acc[:, j * 128 : (j + 1) * 128])

        def into(buf, at):
            def put(j, row, value):
                buf[h, at, j, row : row + 256] = value.astype(BF)

            return put

        product((main + 2) % 4, into(s1, 0))
        far = []
        for j in range(4):
            far.append(comm.send(s1.at[h, 0, j], r1.at[h, j], main_ends[j // 2]))
        yield
        product((main + 1) % 4, into(s2, 0))
        near = {}
        for j in (2, 3):
            near[0, j] = comm.send(s2.at[h, 0, j], r2.at[h, 0, j], main_ends[0])
        product((main + 3) % 4, into(s2, 1))
        for j in (0, 1):
            near[1, j] = comm.send(s2.at[h, 1, j], r2.at[h, 1, j], main_ends[1])
        yield

        def put_own(j, row, value):
            own[h, j, row : row + 256] = value

        product(main, put_own)
        yield
        for a, b in ((0, 2), (1, 3)):
            far[a].wait_recv()
            s2[h, 0, a] = (s2[h, 0, a].astype(F32) + r1[h, a].astype(F32)).astype(BF)
            near[0, a] = comm.send(s2.at[h, 0, a], r2.at[h, 0, a], main_ends[0])
            far[b].wait_recv()
            s2[h, 1, b] = (s2[h, 1, b].astype(F32) + r1[h, b].astype(F32)).astype(BF)
            near[1, b] = comm.send(s2.at[h, 1, b], r2.at[h, 1, b], main_ends[1])
        yield
        for key in ((0, 2), (0, 3), (1, 0), (1, 1), (0, 0), (1, 2), (0, 1), (1, 3)):
            near[key].wait_recv()
        yield

        def summed(j):
            return own[h, j] + r2[h, 0, j].astype(F32) + r2[h, 1, j].astype(F32)

        t1[h] = summed((side + 2) % 4).astype(BF)
        last_far = (
            comm.send(t1.at[h, 0:512], u1.at[h, 0], side_ends[0]),
            comm.send(t1.at[h, 512:1024], u1.at[h, 1], side_ends[1]),
        )
        yield
        part_up = summed((side + 1) % 4)
        part_down = summed((side + 3) % 4)
        t2[h, 0, 512:1024] = part_up[512:1024].astype(BF)
        t2[h, 1, 0:512] = part_down[0:512].astype(BF)
        early = (
            comm.send(t2.at[h, 0, 512:1024], u2.at[h, 0, 512:1024], side_ends[0]),
            comm.send(t2.at[h, 1, 0:512], u2.at[h, 1, 0:512], side_ends[1]),
        )
        last_far[0].wait_recv()
        t2[h, 0, 0:512] = (part_up[0:512] + u1[h, 0].astype(F32)).astype(BF)
        last = [comm.send(t2.at[h, 0, 0:512], u2.at[h, 0, 0:512], side_ends[0])]
        last_far[1].wait_recv()
        t2[h, 1, 512:1024] = (part_down[512:1024] + u1[h, 1].astype(F32)).astype(BF)
        last.append(comm.send(t2.at[h, 1, 512:1024], u2.at[h, 1, 512:1024], side_ends[1]))
        yield
        part = summed(side)
        for copy in (*early, *last):
            copy.wait_recv()
        mixed[h * 1024 : (h + 1) * 1024] = (
            part + u2[h, 0].astype(F32) + u2[h, 1].astype(F32)
        )

    run(rs_half(0, y, ye, x, xe), rs_half(1, x, xe, y, ye))

    lane = lax.broadcasted_iota(jnp.int32, (16, 128), 1)
    row = lax.broadcasted_iota(jnp.int32, (16, 128), 0)
    is_path = lane < 64
    taps = [cw_ref[i : i + 1] for i in range(CONV)]
    bias = cb_ref[...]

    def strided(j):
        return mixed[pl.ds(j, 16, stride=128), :]

    def before(j):
        return jnp.where(row == 0, 0.0, pltpu.roll(strided(j), 1, 0))

    def conv_step(j, carried):
        older, old, recent = carried
        now = strided(j)
        total = bias + taps[0] * older + taps[1] * old + taps[2] * recent + taps[3] * now
        value = jnp.where(is_path, total, now)
        uz_ref[pl.ds(pl.multiple_of(j * 16, 16), 16), :] = value / (1.0 + jnp.exp(-value))
        return (old, recent, now)

    lax.fori_loop(0, 128, conv_step, (before(125), before(126), before(127)), unroll=4)

    zeros = jnp.zeros((64, 256), BF)
    rank_weight = jnp.concatenate([pw_ref[:, 0:256], zeros], axis=0)
    map_weight = jnp.transpose(pw_ref[:, 256:272].astype(F32))
    map_weight = jnp.concatenate([map_weight, jnp.zeros((16, 64), F32)], axis=1).astype(BF)

    def local_block(tb):
        u = uz_ref[pl.ds(pl.multiple_of(tb * 256, 256), 256), :].astype(BF)
        gs[tb, 0:256] = mm(u, rank_weight).astype(BF)
        gs[tb, 256:272] = nt_dot(map_weight, u).astype(BF)

    crossing = []
    for off in offsets:
        zt = (z + off) % 4
        local_block(4 * o + zt)
        crossing.append(comm.send(gs.at[4 * o + zt], gr.at[zt], sib))
    near = []
    for at, off in enumerate(offsets):
        zt = (z + off) % 4
        local_block(4 * k + zt)
        crossing[at].wait_recv()
        part = gs[4 * k + zt].astype(F32) + gr[zt].astype(F32)
        if off == 2:
            gz[0, 0] = part[:, 0:128].astype(BF)
            gz[0, 1] = part[:, 128:256].astype(BF)
            far = (
                comm.send(gz.at[0, 0], gzf.at[0], ze[0]),
                comm.send(gz.at[0, 1], gzf.at[1], ze[1]),
            )
        elif off == 1:
            far[0].wait_recv()
            gz[1, 0] = (part[:, 0:128] + gzf[0].astype(F32)).astype(BF)
            gz[1, 1] = part[:, 128:256].astype(BF)
            near.append(comm.send(gz.at[1], gzn.at[0], ze[0]))
        elif off == 3:
            far[1].wait_recv()
            gz[2, 0] = part[:, 0:128].astype(BF)
            gz[2, 1] = (part[:, 128:256] + gzf[1].astype(F32)).astype(BF)
            near.append(comm.send(gz.at[2], gzn.at[1], ze[1]))
        else:
            near[0].wait_recv()
            near[1].wait_recv()
            left, right = gzn[0].astype(F32), gzn[1].astype(F32)
            gx[0, 0, x] = (part[:, 0:128] + left[0] + right[0]).astype(BF)
            gx[1, 0, y] = (part[:, 128:256] + left[1] + right[1]).astype(BF)

    def sum_half(h, axes):
        for step, (mine, ends) in enumerate(axes):

            def place(d, start, count):
                return gx.at[h, step, (mine + d) % 4, pl.ds(start, count)]

            yield from ring_gather(comm, place, ROWS, SPLIT, ends)
            total = gx[h, step, 0].astype(F32)
            for at in range(1, 4):
                total = total + gx[h, step, at].astype(F32)
            if step == 0:
                gx[h, 1, axes[1][0]] = total.astype(BF)
            else:
                gfull[4 * k + z, :, h * 128 : (h + 1) * 128] = total.astype(BF)
            yield

    run(sum_half(0, ((x, xe), (y, ye))), sum_half(1, ((y, ye), (x, xe))))

    across = []

    def g_place(d, start, count):
        return gfull.at[4 * k + (z + d) % 4, pl.ds(start, count)]

    def g_also(d):
        block = gfull.at[4 * k + (z + d) % 4]
        across.append(comm.send(block, block, sib))

    run(ring_gather(comm, g_place, ROWS, SPLIT, ze, g_also))
    for copy in across:
        copy.wait_recv()
    g_ref[...] = gfull[...]
    comm.finish()


def front(queries, keys, values, residual, out_weight, gain, weights, cw, cb, pw):
    vmem = pl.BlockSpec(memory_space=pltpu.VMEM)
    anyspace = pl.BlockSpec(memory_space=pl.ANY)
    copies = 320
    return pl.pallas_call(
        front_kernel,
        out_shape=(
            jax.ShapeDtypeStruct((2048, 128), F32),
            jax.ShapeDtypeStruct((8, ROWS, 256), BF),
        ),
        in_specs=[vmem, vmem, vmem, anyspace, vmem, vmem, anyspace, vmem, vmem, vmem],
        out_specs=(vmem, vmem),
        scratch_shapes=[
            pltpu.VMEM((4, 4, 128, 256), BF),
            pltpu.VMEM((4, 4, 128, 512), BF),
            pltpu.VMEM((4, 256, 512), BF),
            pltpu.VMEM((4, 256, 512), BF),
            pltpu.VMEM((3, 256, 512), BF),
            pltpu.VMEM((2, 256, 512), BF),
            pltpu.VMEM((2, 128, 512), BF),
            pltpu.VMEM((2, 4, 256, 512), BF),
            pltpu.VMEM((256, 512), F32),
            pltpu.VMEM((8, 256), F32),
            pltpu.VMEM((16, 8, 256), F32),
            pltpu.VMEM((256, 512), BF),
            pltpu.VMEM((2, 16, 64, 512), BF),
            pltpu.VMEM((2, 1, 4, 1024, 128), BF),
            pltpu.VMEM((2, 4, 1024, 128), BF),
            pltpu.VMEM((2, 2, 4, 1024, 128), BF),
            pltpu.VMEM((2, 2, 4, 1024, 128), BF),
            pltpu.VMEM((2, 4, 1024, 128), F32),
            pltpu.VMEM((2, 1024, 128), BF),
            pltpu.VMEM((2, 2, 512, 128), BF),
            pltpu.VMEM((2, 2, 1024, 128), BF),
            pltpu.VMEM((2, 2, 1024, 128), BF),
            pltpu.VMEM((2048, 128), F32),
            pltpu.VMEM((8, ROWS, 256), BF),
            pltpu.VMEM((4, ROWS, 256), BF),
            pltpu.VMEM((3, 2, ROWS, 128), BF),
            pltpu.VMEM((2, 2, ROWS, 128), BF),
            pltpu.VMEM((2, ROWS, 128), BF),
            pltpu.VMEM((2, 2, 4, ROWS, 128), BF),
            pltpu.VMEM((8, ROWS, 256), BF),
            pltpu.SemaphoreType.DMA((copies,)),
            pltpu.SemaphoreType.DMA((copies,)),
            pltpu.SemaphoreType.DMA((2,)),
        ],
        compiler_params=pltpu.CompilerParams(
            collective_id=0, has_side_effects=True, vmem_limit_bytes=60 * 1024 * 1024
        ),
        name="front",
    )(queries, keys, values, residual, out_weight, gain, weights, cw, cb, pw)


def tail_kernel(uz_ref, g_ref, dtw_ref, dtb_ref, al_ref, skip_ref, out_ref, step, wide, drive, ys):
    lane8 = lax.broadcasted_iota(jnp.int32, (16, 1024), 1)
    row8 = lax.broadcasted_iota(jnp.int32, (16, 1024), 0)
    state = 2 * ((lane8 // 128) % 4) + (lane8 % 128) // 64 + 8 * (lane8 // 512)
    spread = jnp.where(row8 == state, 1.0, 0.0).astype(BF)
    dtw = jnp.concatenate([dtw_ref[...], dtw_ref[...]], axis=0)
    dtb = dtb_ref[...]
    lane = lax.broadcasted_iota(jnp.int32, (256, 128), 1)
    low = lane < 64
    for tb in range(8):
        rows = pl.ds(tb * 256, 256)
        pre = nt_dot(g_ref[tb, 0:256], dtw) + dtb
        st = jnp.maximum(pre, 0.0) + jnp.log1p(jnp.exp(-jnp.abs(pre)))
        step[rows] = st
        u = uz_ref[rows].astype(BF).astype(F32)
        u = jnp.where(low, u, pltpu.roll(u, 64, 1))
        drive[rows] = st * u
        wide[rows] = lax.dot_general(
            g_ref[tb, 256:272], spread, TN, preferred_element_type=F32
        )
    low_row = lax.broadcasted_iota(jnp.int32, (1, 128), 1) < 64
    decay = []
    for q in range(4):
        both = jnp.where(low_row, al_ref[2 * q : 2 * q + 1], al_ref[2 * q + 1 : 2 * q + 2])
        decay.append(-jnp.exp(both) * LOG2E)
    row = lax.broadcasted_iota(jnp.int32, (16, 128), 0)
    nothing = jnp.zeros((16, 128), F32)

    def advance(j, states):
        at = pl.ds(pl.multiple_of(j * 16, 16), 16)
        st = step[at]
        du = drive[at]
        return st, tuple(
            jnp.exp2(st * decay[q]) * states[q] + du * wide[at, q * 128 : (q + 1) * 128]
            for q in range(4)
        )

    def first_pass(j, carried):
        total, states = carried
        st, states = advance(j, states)
        return (total + st, states)

    total, ends = lax.fori_loop(0, 128, first_pass, (nothing, (nothing,) * 4), unroll=4)

    entry = []
    for q in range(4):
        factor = jnp.exp2(total * decay[q])
        value = ends[q]
        for d in (1, 2, 4, 8):
            moved_factor = jnp.where(row < d, 1.0, pltpu.roll(factor, d, 0))
            moved_value = jnp.where(row < d, 0.0, pltpu.roll(value, d, 0))
            value = factor * moved_value + value
            factor = factor * moved_factor
        entry.append(jnp.where(row < 1, 0.0, pltpu.roll(value, 1, 0)))

    skip = skip_ref[...]

    def second_pass(j, states):
        _, states = advance(j, states)
        at = pl.ds(pl.multiple_of(j * 16, 16), 16)
        uz = uz_ref[at]
        read = states[0] * wide[at, 512:640]
        for q in range(1, 4):
            read = read + states[q] * wide[at, 512 + q * 128 : 640 + q * 128]
        read = read + pltpu.roll(read, 64, 1)
        u = uz.astype(BF).astype(F32)
        ys[pl.ds(j, 16, stride=128), :] = (read + skip * u) * pltpu.roll(uz, 64, 1)
        return states

    lax.fori_loop(0, 128, second_pass, tuple(entry), unroll=4)
    for seg in range(16):
        block = jnp.transpose(ys[seg * 128 : (seg + 1) * 128, :])
        out_ref[:, seg * 128 : (seg + 1) * 128] = block[0:64].astype(BF)


def tail(uz, g, dtw, dtb, al, skip):
    vmem = pl.BlockSpec(memory_space=pltpu.VMEM)
    return pl.pallas_call(
        tail_kernel,
        out_shape=jax.ShapeDtypeStruct((64, 2048), BF),
        in_specs=[vmem] * 6,
        out_specs=vmem,
        scratch_shapes=[
            pltpu.VMEM((2048, 128), F32),
            pltpu.VMEM((2048, 1024), F32),
            pltpu.VMEM((2048, 128), F32),
            pltpu.VMEM((2048, 128), F32),
        ],
        compiler_params=pltpu.CompilerParams(vmem_limit_bytes=40 * 1024 * 1024),
        name="tail",
    )(uz, g, dtw, dtb, al, skip)


def twice(row):
    return jnp.concatenate([row, row], axis=-1)


def body(
    queries, keys, values, residual, out_weight, norm_gain, in_weight, conv_weight, conv_bias,
    proj_weight, dt_weight, dt_bias, a_log, skip_gain,
):
    uz, g = front(
        queries, keys, values, residual, out_weight, norm_gain[None, :],
        jnp.transpose(in_weight, (1, 2, 3, 0)),
        twice(conv_weight.T), twice(conv_bias[None, :]), proj_weight,
    )
    return tail(
        uz, g, dt_weight.T, twice(dt_bias[None, :]), twice(a_log.T), twice(skip_gain[None, :])
    )


def solution(mesh):
    return jax.shard_map(
        body,
        mesh=mesh,
        in_specs=(
            P("seq", "section"),
            P("seq", "section"),
            P("seq", "section"),
            P(None, "seq"),
            P("section", "seq"),
            P("seq"),
            P("seq", None, None, "section"),
            P(("seq", "section"), None),
            P(("seq", "section")),
            P(("seq", "section"), None),
            P(None, ("seq", "section")),
            P(("seq", "section")),
            P(("seq", "section"), None),
            P(("seq", "section")),
        ),
        out_specs=P(("seq", "section"), None),
        check_vma=False,
    )
```

time: 671 us -> 189 us (0.28)
  waiting for transfers between devices: 413 us -> 0 us
  Pallas kernels: 0 us -> 181 us
  local copies, waits for them, and re-layouts: 95.4 us -> 2.47 us
  blocking collectives: 71.1 us -> 0 us
  other arithmetic: 46.1 us -> 4.44 us
  matrix products: 19.7 us -> 0 us
  between operations: 13.3 us -> 0.03 us
  loops' own time: 9.46 us -> 0 us
    psum x2 -> x0, waiting for transfers between devices: 216 us -> none  [the longest x1 151 us: body(): projected = lax.psum(local_proj, ('seq', 'section'))]
    pallas_call x0 -> x2, Pallas kernels: none -> 181 us  [the longest x1 174 us: front(): pl.pallas_call(front_kernel, out_shape=(jax.ShapeDtypeStruct((2048, 128),...]
    unnamed x5 -> x0, waiting for transfers between devices: 143 us -> none
    pad x384 -> x0, local copies, waits for them, and re-layouts: 60.6 us -> none  [scan_block(): lax.associative_scan(combine, (factor, source), axis=2)]
    all_gather x1 -> x0, waiting for transfers between devices: 54.1 us -> none  [body(): lax.all_gather(attended, 'seq', axis=0, tiled=True)]
    all_gather x2 -> x0, blocking collectives: 37.5 us -> none  [the longest x1 20.1 us: body(): key_part = lax.all_gather(keys, 'seq', axis=0, tiled=True)]
    psum x1 -> x0, blocking collectives: 33.6 us -> none  [body(): squares = lax.psum(jnp.sum(hidden * hidden, axis=1), 'seq')]
    mul x224 -> x0, other arithmetic: 20.5 us -> none  [the longest x32 15.7 us: scan_block(): source = (step_block * input_block)[:, None, :] * in_block[None, :, :]]
  transfers between devices with their start and end apart: 4 -> 0, of which waited for: 4 -> 0; matrix products, arithmetic and copies ran while one was open for 0% -> 0% of each run, Pallas kernels for 0% -> 0%
where the time goes in v1:
time: 189 us; the launch traced here: 188 us
  Pallas kernels  181 us (96%)
  other arithmetic  4.44 us (2%)
  local copies, waits for them, and re-layouts  2.47 us (1%)
    pallas_call x1, Pallas kernels, front(): pl.pallas_call(front_kernel, out_shape=(jax.ShapeDtypeStruct((2048, 128),...  174 us
    pallas_call x1, Pallas kernels, tail(): pl.pallas_call(tail_kernel, out_shape=jax.ShapeDtypeStruct((64, 2048), BF...  7.05 us
    concatenate x4, other arithmetic, twice(): return jnp.concatenate([row, row], axis=-1)  4.44 us

profile of v1, /device:TPU:1, one launch (start us, length us, event | category | flops | bytes accessed | tf_op | source)
XLA Modules:
  0.0 188.0 jit_solution(18373788478352145406)
XLA Ops:
  0.0 1.4 pad_maximum_fusion.2.cb_ref
  1.4 0.8 pad_maximum_fusion.3
  2.2 1.4 pad_maximum_fusion.1.cw_ref
  3.6 0.8 pad_maximum_fusion.al_ref
  4.4 0.0 copy-start.2
  4.4 174.1 %front.1 = (f32[2048,128]{1,0:T(8,128)}, bf16[8,272,256]{2,1,0:T(8,128)(2,1)}) custom-call(bf16[128,512]{1,0:T(8,128)(2,1)} %q_ref.1, bf16[128,128]{1,0:T(8,128)(2,1)} %k_ref.1, bf16[128,128]{1,0:T(8,128)(2,1)} %v_ref.1, bf16[2048,512]{1,0:T(8,128)(2,1)} %res_ref.1, bf16[512,512]{1,0:T(8,128)(2,1)} %ow_ref.1, f32[1,512]{1,0:T(1,128)} %bitcast.11, ...), custom_call_target="tpu_custom_call" | custom-call | tf_op jit(solution)/shard_map/front/pallas_call | solution.py:468
  178.5 0.0 copy-done.2
  178.5 0.0 copy-start
  178.5 1.2 copy-done
  179.8 0.0 copy-start.1
  179.8 1.2 copy-done.1
  181.0 7.1 %tail.1 = bf16[64,2048]{1,0:T(8,128)(2,1)} custom-call(f32[2048,128]{1,0:T(8,128)S(1)} %copy-done.1, bf16[8,272,256]{2,1,0:T(8,128)(2,1)S(1)} %copy-done, bf16[64,256]{1,0:T(8,128)(2,1)S(1)} %bitcast.8, f32[1,128]{1,0:T(1,128)S(1)} %get-tuple-element.9.dtb_ref, f32[8,128]{1,0:T(8,128)S(1)} %pad_maximum_fusion.al_ref, f32[1,128]{1,0:T(1,128)S(1)} %get-tuple-element.10.skip_ref), custom_call_target="tpu_custom_call" | custom-call | tf_op jit(solution)/shard_map/tail/pallas_call | solution.py:595
Async XLA Ops:
  4.4 174.1 %copy-start.2 = (bf16[256,64]{0,1:T(8,128)(2,1)S(1)}, bf16[256,64]{0,1:T(8,128)(2,1)}, u32[]{:S(2)}) copy-start(bf16[256,64]{0,1:T(8,128)(2,1)} %param.24) | copy-start | bytes 98308
  178.5 1.2 copy-start
  179.8 1.2 copy-start.1

commit v2 on v1

v2 whole, which is shorter than its diff:
```python
import math

import jax
import jax.numpy as jnp
from jax import lax
from jax.experimental import pallas as pl
from jax.experimental.pallas import tpu as pltpu
from jax.sharding import PartitionSpec as P

D = 8192
HD = 128
GROUP = 4
NST = 8
DT_RANK = 256
CONV = 4
NORM_EPS = 1e-05
MESH = pl.DeviceIdType.MESH
BF = jnp.bfloat16
F32 = jnp.float32
ROWS = 144
SPLIT = 80
ORDER = (0, -1, 1, 2)
LOG2E = math.log2(math.e)
NT = (((1,), (1,)), ((), ()))
TN = (((0,), (0,)), ((), ()))


def nt_dot(a, b, **kw):
    return lax.dot_general(a, b, NT, preferred_element_type=F32, **kw)


def mm(a, b):
    return jnp.dot(a, b, preferred_element_type=F32)


class Comm:
    def __init__(self, send_sem, recv_sem):
        self.send_sem = send_sem
        self.recv_sem = recv_sem
        self.copies = []

    def send(self, src, dst, dev):
        at = len(self.copies)
        copy = pltpu.make_async_remote_copy(
            src_ref=src,
            dst_ref=dst,
            send_sem=self.send_sem.at[at],
            recv_sem=self.recv_sem.at[at],
            device_id=dev,
            device_id_type=MESH,
        )
        copy.start()
        self.copies.append(copy)
        return copy

    def finish(self):
        for copy in self.copies:
            copy.wait_send()


def run(*streams):
    live = list(streams)
    while live:
        for stream in list(live):
            try:
                next(stream)
            except StopIteration:
                live.remove(stream)


def gather_plane(comm, place, size, first, second):
    half = size // 2
    one = comm.send(place(0, 0, 0, size), place(0, 0, 0, size), first[0])
    two = comm.send(place(0, 0, 0, size), place(0, 0, 0, size), first[1])

    def along(df):
        block = place(df, 0, 0, size)
        return comm.send(block, block, second[0]), comm.send(block, block, second[1])

    sent = [(0, along(0))]
    yield
    one.wait_recv()
    block = place(-1, 0, 0, half)
    three = comm.send(block, block, first[0])
    two.wait_recv()
    block = place(1, 0, half, size - half)
    four = comm.send(block, block, first[1])
    sent.append((-1, along(-1)))
    sent.append((1, along(1)))
    yield
    three.wait_recv()
    four.wait_recv()
    sent.append((2, along(2)))
    yield
    last = []
    for df, (up, down) in sent:
        up.wait_recv()
        block = place(df, -1, 0, half)
        last.append(comm.send(block, block, second[0]))
        down.wait_recv()
        block = place(df, 1, half, size - half)
        last.append(comm.send(block, block, second[1]))
    yield
    for copy in last:
        copy.wait_recv()


def ring_gather(comm, place, size, cut, ends, also=None):
    whole = place(0, 0, size)
    up = comm.send(whole, whole, ends[0])
    down = comm.send(whole, whole, ends[1])
    if also:
        also(0)
    yield
    up.wait_recv()
    block = place(-1, 0, cut)
    far_up = comm.send(block, block, ends[0])
    if also:
        also(-1)
    down.wait_recv()
    block = place(1, cut, size - cut)
    far_down = comm.send(block, block, ends[1])
    if also:
        also(1)
    yield
    far_up.wait_recv()
    far_down.wait_recv()
    if also:
        also(2)


def front_kernel(
    q_ref, k_ref, v_ref, res_ref, ow_ref, gain_ref, w_ref, cw_ref, cb_ref, pw_ref,
    dtw_ref, dtb_ref, al_ref, skip_ref,
    out_ref,
    kv, att, cs, cr, zs, zn, zf, act, hid, ssq_out, ssq_in, inv, res, wv,
    s1, r1, s2, r2, own, t1, u1, t2, u2, mixed, uz,
    gs, gr, gz, gzn, gzf, gx, gfull,
    step_size, wide, drive, ys,
    send_sem, recv_sem, local_sem,
):
    s = lax.axis_index("seq")
    c = lax.axis_index("section")
    x, y = s // 4, s % 4
    z, k = c // 2, c % 2
    o = 1 - k

    def seq_of(cx, cy):
        return {"seq": cx * 4 + cy}

    def section_of(cz, ck):
        return {"section": cz * 2 + ck}

    xe = (seq_of((x + 1) % 4, y), seq_of((x + 3) % 4, y))
    ye = (seq_of(x, (y + 1) % 4), seq_of(x, (y + 3) % 4))
    ze = (section_of((z + 1) % 4, k), section_of((z + 3) % 4, k))
    sib = section_of(z, o)

    res_copy = pltpu.make_async_copy(
        res_ref.at[pl.ds(1024 * k + 256 * z, 256)], res, local_sem.at[0]
    )
    res_copy.start()
    w_copy = pltpu.make_async_copy(w_ref, wv, local_sem.at[1])
    w_copy.start()

    barrier = pltpu.get_barrier_semaphore()
    for off in range(1, 16):
        pl.semaphore_signal(
            barrier, inc=1, device_id={"seq": (s + off) % 16}, device_id_type=MESH
        )
    for off in range(1, 8):
        pl.semaphore_signal(
            barrier, inc=1, device_id={"section": (c + off) % 8}, device_id_type=MESH
        )
    kv[x, y, :, 0:HD] = k_ref[...]
    kv[x, y, :, HD:] = v_ref[...]
    pl.semaphore_wait(barrier, 22)

    comm = Comm(send_sem, recv_sem)

    def plane_place(buf, x_first, base, by_rows=True):
        def place(df, ds, start, count):
            if x_first:
                cx, cy = (x + df) % 4, (y + ds) % 4
            else:
                cx, cy = (x + ds) % 4, (y + df) % 4
            return buf.at[cx, cy, pl.ds(base + start, count)]

        return place

    run(
        gather_plane(comm, plane_place(kv, True, 0), 64, xe, ye),
        gather_plane(comm, plane_place(kv, False, 64), 64, ye, xe),
    )

    query_pos = s * 128 + lax.broadcasted_iota(jnp.int32, (128, 2048), 0)
    key_pos = lax.broadcasted_iota(jnp.int32, (128, 2048), 1)
    allowed = query_pos >= key_pos
    key_rows = kv[:, :, :, 0:HD].reshape(2048, HD)
    value_rows = kv[:, :, :, HD:].reshape(2048, HD)
    for g in range(GROUP):
        scores = nt_dot(q_ref[:, g * HD : (g + 1) * HD], key_rows)
        scores = jnp.where(allowed, scores, -1e30)
        top = jnp.max(scores, axis=1, keepdims=True)
        terms = jnp.exp2((scores - top) * (LOG2E / math.sqrt(HD)))
        total = jnp.sum(terms, axis=1, keepdims=True)
        moved = mm(terms.astype(BF), value_rows)
        att[x, y, :, g * HD : (g + 1) * HD] = (moved / total).astype(BF)

    run(
        gather_plane(comm, plane_place(att, True, 0), 64, xe, ye),
        gather_plane(comm, plane_place(att, False, 64), 64, ye, xe),
    )

    def branch(kk, zt):
        rows = att[2 * kk + zt // 2, pl.ds((zt % 2) * 2, 2)].reshape(256, 512)
        return mm(rows, ow_ref[...])

    offsets = (2, 1, 3, 0)
    crossing = []
    for off in offsets:
        zt = (z + off) % 4
        cs[zt] = branch(o, zt).astype(BF)
        crossing.append(comm.send(cs.at[zt], cr.at[zt], sib))
    w_copy.wait()
    res_copy.wait()
    near = []
    for at, off in enumerate(offsets):
        zt = (z + off) % 4
        part = branch(k, zt)
        crossing[at].wait_recv()
        part = part + cr[zt].astype(F32)
        if off == 2:
            zs[0] = part.astype(BF)
            far = (
                comm.send(zs.at[0, 0:128], zf.at[0], ze[0]),
                comm.send(zs.at[0, 128:256], zf.at[1], ze[1]),
            )
        elif off == 1:
            far[0].wait_recv()
            zs[1, 0:128] = (part[0:128] + zf[0].astype(F32)).astype(BF)
            zs[1, 128:256] = part[128:256].astype(BF)
            near.append(comm.send(zs.at[1], zn.at[0], ze[0]))
        elif off == 3:
            far[1].wait_recv()
            zs[2, 0:128] = part[0:128].astype(BF)
            zs[2, 128:256] = (part[128:256] + zf[1].astype(F32)).astype(BF)
            near.append(comm.send(zs.at[2], zn.at[1], ze[1]))
        else:
            part = part + res[...].astype(F32)
            near[0].wait_recv()
            part = part + zn[0].astype(F32)
            near[1].wait_recv()
            hid[...] = part + zn[1].astype(F32)

    hidden = hid[...]
    act[k, z] = (hidden * gain_ref[...]).astype(BF)
    across = []

    def act_place(d, start, count):
        return act.at[k, (z + d) % 4, pl.ds(start, count)]

    def act_also(d):
        block = act.at[k, (z + d) % 4]
        across.append(comm.send(block, block, sib))

    def gather_act():
        yield from ring_gather(comm, act_place, 256, 128, ze, act_also)

    act_steps = gather_act()
    next(act_steps)
    ssq_out[...] = nt_dot(jnp.ones((8, 512), F32), hidden * hidden, precision=lax.Precision.HIGHEST)
    ssq_in[s] = ssq_out[...]
    squares = [
        comm.send(ssq_out, ssq_in.at[s], {"seq": (s + off) % 16}) for off in range(1, 16)
    ]
    inverses = []

    def share_inverse():
        for copy in squares:
            copy.wait_recv()
        total = ssq_in[0]
        for at in range(1, 16):
            total = total + ssq_in[at]
        inv[k, z] = lax.rsqrt(total / D + NORM_EPS)
        for dz in range(4):
            for flip in range(2):
                if dz or flip:
                    to = section_of((z + dz) % 4, (k + flip) % 2)
                    inverses.append(comm.send(inv.at[k, z], inv.at[k, z], to))

    def unit(u):
        ch = u // 4
        zt = (z + ORDER[u % 4]) % 4
        by_y = u % 2 == 0
        main, main_ends, side, side_ends = (y, ye, x, xe) if by_y else (x, xe, y, ye)

        def product(p):
            rows = []
            for j in range(4):
                b = (j * 4 + p) if by_y else (p * 4 + j)
                rows += [wv[0, b], wv[1, b]]
            return nt_dot(act[ch, zt], jnp.concatenate(rows, axis=0))

        acc = product((main + 2) % 4)
        for j in range(4):
            s1[u, j] = acc[:, j * 128 : (j + 1) * 128].astype(BF)
        far = [
            comm.send(s1.at[u, 2 * e : 2 * e + 2], r1.at[u, 2 * e : 2 * e + 2], main_ends[e])
            for e in range(2)
        ]
        yield
        early, late = [], []
        for e, step in ((0, 1), (1, 3)):
            acc = product((main + step) % 4)
            for j in range(4):
                s2[u, e, j] = acc[:, j * 128 : (j + 1) * 128].astype(BF)
            span = pl.ds(2 - 2 * e, 2)
            early.append(comm.send(s2.at[u, e, span], r2.at[u, e, span], main_ends[e]))
        yield
        acc = product(main)
        for j in range(4):
            own[u, j] = acc[:, j * 128 : (j + 1) * 128]
        yield
        for e in range(2):
            far[e].wait_recv()
            span = pl.ds(2 * e, 2)
            s2[u, e, span] = (s2[u, e, span].astype(F32) + r1[u, span].astype(F32)).astype(BF)
            late.append(comm.send(s2.at[u, e, span], r2.at[u, e, span], main_ends[e]))
        yield
        for copy in (*early, *late):
            copy.wait_recv()

        def summed(j):
            return own[u, j] + r2[u, 0, j].astype(F32) + r2[u, 1, j].astype(F32)

        def summed_rows(j, rest):
            return (
                own[u, j, rest] + r2[u, 0, j, rest].astype(F32) + r2[u, 1, j, rest].astype(F32)
            )

        t1[u] = summed((side + 2) % 4).astype(BF)
        last_far = [
            comm.send(t1.at[u, 128 * e : 128 * e + 128], u1.at[u, e], side_ends[e])
            for e in range(2)
        ]
        parts = summed((side + 1) % 4), summed((side + 3) % 4)
        last = []
        for e in range(2):
            rest = slice(128 - 128 * e, 256 - 128 * e)
            t2[u, e, rest] = parts[e][rest].astype(BF)
            last.append(comm.send(t2.at[u, e, rest], u2.at[u, e, rest], side_ends[e]))
        yield
        for e in range(2):
            last_far[e].wait_recv()
            rest = slice(128 * e, 128 * e + 128)
            j = (side + 1 + 2 * e) % 4
            part = summed_rows(j, rest) + u1[u, e].astype(F32)
            t2[u, e, rest] = part.astype(BF)
            last.append(comm.send(t2.at[u, e, rest], u2.at[u, e, rest], side_ends[e]))
        yield
        for copy in last:
            copy.wait_recv()
        part = summed(side) + u2[u, 0].astype(F32) + u2[u, 1].astype(F32)
        scale = jnp.transpose(inv[ch, zt])[:, 0:1]
        mixed[pl.ds(pl.multiple_of(ch * 1024 + zt * 256, 256), 256)] = part * scale
        yield

    lane = lax.broadcasted_iota(jnp.int32, (8, 128), 1)
    row = lax.broadcasted_iota(jnp.int32, (8, 128), 0)
    is_path = lane < 64
    low_row = lax.broadcasted_iota(jnp.int32, (1, 128), 1) < 64

    def twice(value):
        return jnp.concatenate([value, value], axis=1)

    taps = twice(cw_ref[...])
    bias = twice(cb_ref[...])

    def conv(ch):
        def strided(j):
            return mixed[pl.ds(ch * 1024 + j, 8, stride=128), :]

        def before(j):
            if ch:
                return mixed[pl.ds(ch * 1024 - 128 + j, 8, stride=128), :]
            return jnp.where(row == 0, 0.0, pltpu.roll(strided(j), 1, 0))

        def step(j, carried):
            older, old, recent = carried
            now = strided(j)
            total = (
                bias + taps[0:1] * older + taps[1:2] * old + taps[2:3] * recent + taps[3:4] * now
            )
            value = jnp.where(is_path, total, now)
            at = pl.ds(pl.multiple_of(ch * 1024 + j * 8, 8), 8)
            uz[at, :] = value / (1.0 + jnp.exp(-value))
            return (old, recent, now)

        lax.fori_loop(0, 128, step, (before(125), before(126), before(127)), unroll=8)

    def sum_maps(ch):
        rank_weight = jnp.concatenate([pw_ref[:, 0:256], jnp.zeros((64, 256), BF)], axis=0)
        map_weight = jnp.transpose(pw_ref[:, 256:272].astype(F32))
        map_weight = jnp.concatenate([map_weight, jnp.zeros((16, 64), F32)], axis=1).astype(BF)

        def local_block(i):
            at = pl.ds(pl.multiple_of(ch * 1024 + i * 128, 128), 128)
            u = uz[at, :].astype(BF)
            gs[ch, i, 0:128] = mm(u, rank_weight).astype(BF)
            maps = nt_dot(map_weight, u).astype(BF)
            gs[ch, i, 128:ROWS] = jnp.concatenate([maps, jnp.zeros((16, 128), BF)], axis=1)

        offs = (2, 1, 3, 0)
        crossing = []
        for off in offs:
            zt = (z + off) % 4
            local_block(4 * o + zt)
            crossing.append(comm.send(gs.at[ch, 4 * o + zt], gr.at[ch, zt], sib))
        yield
        for off in offs:
            local_block(4 * k + (z + off) % 4)
        near = []
        for at, off in enumerate(offs):
            zt = (z + off) % 4
            crossing[at].wait_recv()
            part = gs[ch, 4 * k + zt].astype(F32) + gr[ch, zt].astype(F32)
            left, right = part[:, 0:128], part[:, 128:256]
            if off == 2:
                gz[ch, 0, 0] = left.astype(BF)
                gz[ch, 0, 1] = right.astype(BF)
                far = [comm.send(gz.at[ch, 0, e], gzf.at[ch, e], ze[e]) for e in range(2)]
                yield
            elif off == 1:
                far[0].wait_recv()
                gz[ch, 1, 0] = (left + gzf[ch, 0].astype(F32)).astype(BF)
                gz[ch, 1, 1] = right.astype(BF)
                near.append(comm.send(gz.at[ch, 1], gzn.at[ch, 0], ze[0]))
            elif off == 3:
                far[1].wait_recv()
                gz[ch, 2, 0] = left.astype(BF)
                gz[ch, 2, 1] = (right + gzf[ch, 1].astype(F32)).astype(BF)
                near.append(comm.send(gz.at[ch, 2], gzn.at[ch, 1], ze[1]))
                yield
            else:
                near[0].wait_recv()
                near[1].wait_recv()
                down, up = gzn[ch, 0].astype(F32), gzn[ch, 1].astype(F32)
                gx[ch, 0, 0, x] = (left + down[0] + up[0]).astype(BF)
                gx[ch, 1, 0, y] = (right + down[1] + up[1]).astype(BF)

        def sum_half(h, axes):
            for step, (mine, ends) in enumerate(axes):

                def place(d, start, count):
                    return gx.at[ch, h, step, (mine + d) % 4, pl.ds(start, count)]

                yield from ring_gather(comm, place, ROWS, SPLIT, ends)
                total = gx[ch, h, step, 0].astype(F32)
                for at in range(1, 4):
                    total = total + gx[ch, h, step, at].astype(F32)
                if step == 0:
                    gx[ch, h, 1, axes[1][0]] = total.astype(BF)
                else:
                    gfull[ch, 4 * k + z, :, h * 128 : (h + 1) * 128] = total.astype(BF)

        halves = sum_half(0, ((x, xe), (y, ye))), sum_half(1, ((y, ye), (x, xe)))
        live = True
        while live:
            live = False
            for half in halves:
                try:
                    next(half)
                    live = True
                except StopIteration:
                    pass
            if live:
                yield

        across_maps = []

        def place(d, start, count):
            return gfull.at[ch, 4 * k + (z + d) % 4, pl.ds(start, count)]

        def also(d):
            block = gfull.at[ch, 4 * k + (z + d) % 4]
            across_maps.append(comm.send(block, block, sib))

        yield from ring_gather(comm, place, ROWS, SPLIT, ze, also)
        for copy in across_maps:
            copy.wait_recv()

    lane8 = lax.broadcasted_iota(jnp.int32, (16, 1024), 1)
    row8 = lax.broadcasted_iota(jnp.int32, (16, 1024), 0)
    which = 2 * ((lane8 // 128) % 4) + (lane8 % 128) // 64 + 8 * (lane8 // 512)
    spread = jnp.where(row8 == which, 1.0, 0.0).astype(BF)

    def decays():
        al = twice(al_ref[...])
        return [
            -jnp.exp(jnp.where(low_row, al[2 * q : 2 * q + 1], al[2 * q + 1 : 2 * q + 2])) * LOG2E
            for q in range(4)
        ]

    def prepare(ch):
        dtw = jnp.concatenate([dtw_ref[...], dtw_ref[...]], axis=0)
        dtb = twice(dtb_ref[...])
        low = lax.broadcasted_iota(jnp.int32, (128, 128), 1) < 64
        for i in range(8):
            rows = pl.ds(i * 128, 128)
            pre = nt_dot(gfull[ch, i, 0:128], dtw) + dtb
            st = jnp.maximum(pre, 0.0) + jnp.log1p(jnp.exp(-jnp.abs(pre)))
            step_size[rows] = st
            u = uz[pl.ds(ch * 1024 + i * 128, 128)].astype(BF).astype(F32)
            drive[rows] = st * jnp.where(low, u, pltpu.roll(u, 64, 1))
            wide[rows] = lax.dot_general(
                gfull[ch, i, 128:ROWS, 0:128], spread, TN, preferred_element_type=F32
            )

    nothing = jnp.zeros((8, 128), F32)

    def advance(j, states, decay):
        at = pl.ds(pl.multiple_of(j * 8, 8), 8)
        st = step_size[at]
        du = drive[at]
        return st, tuple(
            jnp.exp2(st * decay[q]) * states[q] + du * wide[at, q * 128 : (q + 1) * 128]
            for q in range(4)
        )

    def segment_ends():
        decay = decays()

        def first_pass(j, carried):
            total, states = carried
            st, states = advance(j, states, decay)
            return (total + st, states)

        return lax.fori_loop(0, 128, first_pass, (nothing, (nothing,) * 4), unroll=8)

    def entries(found, carry):
        total, ends = found
        decay = decays()
        starts, after = [], []
        for q in range(4):
            factor = jnp.exp2(total * decay[q])
            value = ends[q]
            for d in (1, 2, 4):
                moved_factor = jnp.where(row < d, 1.0, pltpu.roll(factor, d, 0))
                moved_value = jnp.where(row < d, 0.0, pltpu.roll(value, d, 0))
                value = factor * moved_value + value
                factor = factor * moved_factor
            if carry is not None:
                value = value + factor * carry[q]
            start = pltpu.roll(value, 1, 0)
            starts.append(jnp.where(row < 1, 0.0 if carry is None else carry[q], start))
            after.append(jnp.broadcast_to(value[7:8], (8, 128)))
        return starts, after

    def finish(ch, starts):
        decay = decays()
        skip = twice(skip_ref[...])

        def second_pass(j, states):
            _, states = advance(j, states, decay)
            at = pl.ds(pl.multiple_of(j * 8, 8), 8)
            gated = uz[pl.ds(pl.multiple_of(ch * 1024 + j * 8, 8), 8)]
            read = states[0] * wide[at, 512:640]
            for q in range(1, 4):
                read = read + states[q] * wide[at, 512 + q * 128 : 640 + q * 128]
            read = read + pltpu.roll(read, 64, 1)
            u = gated.astype(BF).astype(F32)
            ys[pl.ds(j, 8, stride=128), :] = (read + skip * u) * pltpu.roll(gated, 64, 1)
            return states

        lax.fori_loop(0, 128, second_pass, tuple(starts), unroll=8)
        for seg in range(8):
            block = jnp.transpose(ys[seg * 128 : (seg + 1) * 128, :])
            column = ch * 1024 + seg * 128
            out_ref[:, column : column + 128] = block[0:64].astype(BF)

    pairs = {}

    def go(pair, steps):
        if pair not in pairs:
            pairs[pair] = (unit(2 * pair), unit(2 * pair + 1))
        for _ in range(steps):
            for stream in pairs[pair]:
                next(stream)

    def advance_all(stream, steps=1):
        for _ in range(steps):
            next(stream, None)

    run(act_steps)
    for copy in across:
        copy.wait_recv()

    go(0, 3)
    share_inverse()
    go(0, 1)
    go(1, 3)
    go(0, 1)
    go(1, 1)
    go(0, 1)
    go(2, 3)
    for copy in inverses:
        copy.wait_recv()
    go(0, 1)
    go(1, 1)
    go(2, 1)
    go(1, 1)
    go(3, 3)
    go(1, 1)
    conv(0)
    maps0 = sum_maps(0)
    advance_all(maps0)
    go(2, 1)
    advance_all(maps0)
    go(3, 1)
    advance_all(maps0)
    go(2, 1)
    advance_all(maps0)
    go(3, 1)
    advance_all(maps0)
    go(2, 1)
    advance_all(maps0)
    go(3, 1)
    advance_all(maps0)
    go(3, 1)

    conv(1)
    maps1 = sum_maps(1)
    advance_all(maps1)
    advance_all(maps0)
    advance_all(maps1)
    for _ in maps0:
        pass
    prepare(0)
    advance_all(maps1)
    found = segment_ends()
    advance_all(maps1)
    starts, carry = entries(found, None)
    finish(0, starts)
    for _ in maps1:
        pass

    prepare(1)
    starts, carry = entries(segment_ends(), carry)
    finish(1, starts)
    comm.finish()


def body(
    queries, keys, values, residual, out_weight, norm_gain, in_weight, conv_weight, conv_bias,
    proj_weight, dt_weight, dt_bias, a_log, skip_gain,
):
    vmem = pl.BlockSpec(memory_space=pltpu.VMEM)
    anyspace = pl.BlockSpec(memory_space=pl.ANY)
    copies = 400
    return pl.pallas_call(
        front_kernel,
        out_shape=jax.ShapeDtypeStruct((64, 2048), BF),
        in_specs=[vmem, vmem, vmem, anyspace, vmem, vmem, anyspace] + [vmem] * 7,
        out_specs=vmem,
        scratch_shapes=[
            pltpu.VMEM((4, 4, 128, 256), BF),
            pltpu.VMEM((4, 4, 128, 512), BF),
            pltpu.VMEM((4, 256, 512), BF),
            pltpu.VMEM((4, 256, 512), BF),
            pltpu.VMEM((3, 256, 512), BF),
            pltpu.VMEM((2, 256, 512), BF),
            pltpu.VMEM((2, 128, 512), BF),
            pltpu.VMEM((2, 4, 256, 512), BF),
            pltpu.VMEM((256, 512), F32),
            pltpu.VMEM((8, 256), F32),
            pltpu.VMEM((16, 8, 256), F32),
            pltpu.VMEM((2, 4, 8, 256), F32),
            pltpu.VMEM((256, 512), BF),
            pltpu.VMEM((2, 16, 64, 512), BF),
            pltpu.VMEM((8, 4, 256, 128), BF),
            pltpu.VMEM((8, 4, 256, 128), BF),
            pltpu.VMEM((8, 2, 4, 256, 128), BF),
            pltpu.VMEM((8, 2, 4, 256, 128), BF),
            pltpu.VMEM((8, 4, 256, 128), F32),
            pltpu.VMEM((8, 256, 128), BF),
            pltpu.VMEM((8, 2, 128, 128), BF),
            pltpu.VMEM((8, 2, 256, 128), BF),
            pltpu.VMEM((8, 2, 256, 128), BF),
            pltpu.VMEM((2048, 128), F32),
            pltpu.VMEM((2048, 128), F32),
            pltpu.VMEM((2, 8, ROWS, 256), BF),
            pltpu.VMEM((2, 4, ROWS, 256), BF),
            pltpu.VMEM((2, 3, 2, ROWS, 128), BF),
            pltpu.VMEM((2, 2, 2, ROWS, 128), BF),
            pltpu.VMEM((2, 2, ROWS, 128), BF),
            pltpu.VMEM((2, 2, 2, 4, ROWS, 128), BF),
            pltpu.VMEM((2, 8, ROWS, 256), BF),
            pltpu.VMEM((1024, 128), F32),
            pltpu.VMEM((1024, 1024), F32),
            pltpu.VMEM((1024, 128), F32),
            pltpu.VMEM((1024, 128), F32),
            pltpu.SemaphoreType.DMA((copies,)),
            pltpu.SemaphoreType.DMA((copies,)),
            pltpu.SemaphoreType.DMA((2,)),
        ],
        compiler_params=pltpu.CompilerParams(
            collective_id=0, has_side_effects=True, vmem_limit_bytes=60 * 1024 * 1024
        ),
        name="front",
    )(
        queries, keys, values, residual, out_weight, norm_gain[None, :],
        jnp.transpose(in_weight, (1, 2, 3, 0)), conv_weight.T, conv_bias[None, :], proj_weight,
        dt_weight.T, dt_bias[None, :], a_log.T, skip_gain[None, :],
    )


def solution(mesh):
    return jax.shard_map(
        body,
        mesh=mesh,
        in_specs=(
            P("seq", "section"),
            P("seq", "section"),
            P("seq", "section"),
            P(None, "seq"),
            P("section", "seq"),
            P("seq"),
            P("seq", None, None, "section"),
            P(("seq", "section"), None),
            P(("seq", "section")),
            P(("seq", "section"), None),
            P(None, ("seq", "section")),
            P(("seq", "section")),
            P(("seq", "section"), None),
            P(("seq", "section")),
        ),
        out_specs=P(("seq", "section"), None),
        check_vma=False,
    )
```

time: 189 us -> 180 us (0.952)
  other arithmetic: 4.44 us -> 0 us
  Pallas kernels: 181 us -> 178 us
    concatenate x4 -> x0, other arithmetic: 4.44 us -> none  [twice(): return jnp.concatenate([row, row], axis=-1)]
    pallas_call x2 -> x1, Pallas kernels: 181 us -> 178 us  [body(): pl.pallas_call(front_kernel, out_shape=jax.ShapeDtypeStruct((64, 2048), B...]
where the time goes in v2:
time: 180 us
  Pallas kernels  178 us (99%)
    pallas_call x1, Pallas kernels, body(): pl.pallas_call(front_kernel, out_shape=jax.ShapeDtypeStruct((64, 2048), B...  178 us

profile of v2, /device:TPU:1, one launch (start us, length us, event | category | flops | bytes accessed | tf_op | source)
XLA Modules:
  0.0 179.9 jit_solution(13490853075231124065)
XLA Ops:
  0.0 178.2 %front.1 = bf16[64,2048]{1,0:T(8,128)(2,1)} custom-call(bf16[128,512]{1,0:T(8,128)(2,1)} %q_ref.1, bf16[128,128]{1,0:T(8,128)(2,1)} %k_ref.1, bf16[128,128]{1,0:T(8,128)(2,1)} %v_ref.1, bf16[2048,512]{1,0:T(8,128)(2,1)} %res_ref.1, bf16[512,512]{1,0:T(8,128)(2,1)} %ow_ref.1, f32[1,512]{1,0:T(1,128)} %bitcast.11, bf16[2,16,64,512]{3,2,1,0:T(8,128)(2,1)} %bitcast.8, ...), custom_call_target="tpu_custom_call" | custom-call | tf_op jit(solution)/shard_map/front/pallas_call | solution.py:661
  178.2 1.7 copy.16

commit v3 on v2

--- a/solution.py
+++ b/solution.py
@@ -17,8 +17,7 @@
 MESH = pl.DeviceIdType.MESH
 BF = jnp.bfloat16
 F32 = jnp.float32
-ROWS = 144
-SPLIT = 80
+CHUNKS = ((0, 1024), (1024, 512), (1536, 512))
 ORDER = (0, -1, 1, 2)
 LOG2E = math.log2(math.e)
 NT = (((1,), (1,)), ((), ()))
@@ -105,37 +104,13 @@
         copy.wait_recv()
 
 
-def ring_gather(comm, place, size, cut, ends, also=None):
-    whole = place(0, 0, size)
-    up = comm.send(whole, whole, ends[0])
-    down = comm.send(whole, whole, ends[1])
-    if also:
-        also(0)
-    yield
-    up.wait_recv()
-    block = place(-1, 0, cut)
-    far_up = comm.send(block, block, ends[0])
-    if also:
-        also(-1)
-    down.wait_recv()
-    block = place(1, cut, size - cut)
-    far_down = comm.send(block, block, ends[1])
-    if also:
-        also(1)
-    yield
-    far_up.wait_recv()
-    far_down.wait_recv()
-    if also:
-        also(2)
-
-
 def front_kernel(
     q_ref, k_ref, v_ref, res_ref, ow_ref, gain_ref, w_ref, cw_ref, cb_ref, pw_ref,
     dtw_ref, dtb_ref, al_ref, skip_ref,
     out_ref,
     kv, att, cs, cr, zs, zn, zf, act, hid, ssq_out, ssq_in, inv, res, wv,
     s1, r1, s2, r2, own, t1, u1, t2, u2, mixed, uz,
-    gs, gr, gz, gzn, gzf, gx, gfull,
+    gs, gd, gx, gfull,
     step_size, wide, drive, ys,
     send_sem, recv_sem, local_sem,
 ):
@@ -255,20 +230,15 @@
 
     hidden = hid[...]
     act[k, z] = (hidden * gain_ref[...]).astype(BF)
-    across = []
-
-    def act_place(d, start, count):
+    def act_block(d, start=0, count=256):
         return act.at[k, (z + d) % 4, pl.ds(start, count)]
 
-    def act_also(d):
-        block = act.at[k, (z + d) % 4]
-        across.append(comm.send(block, block, sib))
-
-    def gather_act():
-        yield from ring_gather(comm, act_place, 256, 128, ze, act_also)
-
-    act_steps = gather_act()
-    next(act_steps)
+    def pass_on(d, dev, start=0, count=256):
+        block = act_block(d, start, count)
+        return comm.send(block, block, dev)
+
+    act_up, act_down = pass_on(0, ze[0]), pass_on(0, ze[1])
+    across = {0: pass_on(0, sib)}
     ssq_out[...] = nt_dot(jnp.ones((8, 512), F32), hidden * hidden, precision=lax.Precision.HIGHEST)
     ssq_in[s] = ssq_out[...]
     squares = [
@@ -291,7 +261,7 @@
 
     def unit(u):
         ch = u // 4
-        zt = (z + ORDER[u % 4]) % 4
+        zt = u % 4 if ch else (z + ORDER[u]) % 4
         by_y = u % 2 == 0
         main, main_ends, side, side_ends = (y, ye, x, xe) if by_y else (x, xe, y, ye)
 
@@ -378,12 +348,15 @@
     bias = twice(cb_ref[...])
 
     def conv(ch):
+        first, count = CHUNKS[ch]
+        length = count // 8
+
         def strided(j):
-            return mixed[pl.ds(ch * 1024 + j, 8, stride=128), :]
+            return mixed[pl.ds(first + j, 8, stride=length), :]
 
         def before(j):
-            if ch:
-                return mixed[pl.ds(ch * 1024 - 128 + j, 8, stride=128), :]
+            if first:
+                return mixed[pl.ds(first - length + j, 8, stride=length), :]
             return jnp.where(row == 0, 0.0, pltpu.roll(strided(j), 1, 0))
 
         def step(j, carried):
@@ -393,102 +366,77 @@
                 bias + taps[0:1] * older + taps[1:2] * old + taps[2:3] * recent + taps[3:4] * now
             )
             value = jnp.where(is_path, total, now)
-            at = pl.ds(pl.multiple_of(ch * 1024 + j * 8, 8), 8)
+            at = pl.ds(pl.multiple_of(first + j * 8, 8), 8)
             uz[at, :] = value / (1.0 + jnp.exp(-value))
             return (old, recent, now)
 
-        lax.fori_loop(0, 128, step, (before(125), before(126), before(127)), unroll=8)
+        begin = tuple(before(length - 3 + i) for i in range(3))
+        lax.fori_loop(0, length, step, begin, unroll=8)
 
     def sum_maps(ch):
+        first, count = CHUNKS[ch]
+        n = count // 8
+        whole = pl.ds(0, n + 16)
         rank_weight = jnp.concatenate([pw_ref[:, 0:256], jnp.zeros((64, 256), BF)], axis=0)
         map_weight = jnp.transpose(pw_ref[:, 256:272].astype(F32))
         map_weight = jnp.concatenate([map_weight, jnp.zeros((16, 64), F32)], axis=1).astype(BF)
 
         def local_block(i):
-            at = pl.ds(pl.multiple_of(ch * 1024 + i * 128, 128), 128)
-            u = uz[at, :].astype(BF)
-            gs[ch, i, 0:128] = mm(u, rank_weight).astype(BF)
+            u = uz[pl.ds(pl.multiple_of(first + i * n, n), n), :].astype(BF)
+            gs[ch, i, 0:n] = mm(u, rank_weight).astype(BF)
+            if n < 128:
+                u = jnp.concatenate([u, jnp.zeros((128 - n, 128), BF)], axis=0)
             maps = nt_dot(map_weight, u).astype(BF)
-            gs[ch, i, 128:ROWS] = jnp.concatenate([maps, jnp.zeros((16, 128), BF)], axis=1)
-
-        offs = (2, 1, 3, 0)
-        crossing = []
-        for off in offs:
-            zt = (z + off) % 4
-            local_block(4 * o + zt)
-            crossing.append(comm.send(gs.at[ch, 4 * o + zt], gr.at[ch, zt], sib))
-        yield
-        for off in offs:
-            local_block(4 * k + (z + off) % 4)
-        near = []
-        for at, off in enumerate(offs):
-            zt = (z + off) % 4
-            crossing[at].wait_recv()
-            part = gs[ch, 4 * k + zt].astype(F32) + gr[ch, zt].astype(F32)
-            left, right = part[:, 0:128], part[:, 128:256]
-            if off == 2:
-                gz[ch, 0, 0] = left.astype(BF)
-                gz[ch, 0, 1] = right.astype(BF)
-                far = [comm.send(gz.at[ch, 0, e], gzf.at[ch, e], ze[e]) for e in range(2)]
-                yield
-            elif off == 1:
-                far[0].wait_recv()
-                gz[ch, 1, 0] = (left + gzf[ch, 0].astype(F32)).astype(BF)
-                gz[ch, 1, 1] = right.astype(BF)
-                near.append(comm.send(gz.at[ch, 1], gzn.at[ch, 0], ze[0]))
-            elif off == 3:
-                far[1].wait_recv()
-                gz[ch, 2, 0] = left.astype(BF)
-                gz[ch, 2, 1] = (right + gzf[ch, 1].astype(F32)).astype(BF)
-                near.append(comm.send(gz.at[ch, 2], gzn.at[ch, 1], ze[1]))
-                yield
-            else:
-                near[0].wait_recv()
-                near[1].wait_recv()
-                down, up = gzn[ch, 0].astype(F32), gzn[ch, 1].astype(F32)
-                gx[ch, 0, 0, x] = (left + down[0] + up[0]).astype(BF)
-                gx[ch, 1, 0, y] = (right + down[1] + up[1]).astype(BF)
-
-        def sum_half(h, axes):
-            for step, (mine, ends) in enumerate(axes):
-
-                def place(d, start, count):
-                    return gx.at[ch, h, step, (mine + d) % 4, pl.ds(start, count)]
-
-                yield from ring_gather(comm, place, ROWS, SPLIT, ends)
-                total = gx[ch, h, step, 0].astype(F32)
-                for at in range(1, 4):
-                    total = total + gx[ch, h, step, at].astype(F32)
-                if step == 0:
-                    gx[ch, h, 1, axes[1][0]] = total.astype(BF)
-                else:
-                    gfull[ch, 4 * k + z, :, h * 128 : (h + 1) * 128] = total.astype(BF)
-
-        halves = sum_half(0, ((x, xe), (y, ye))), sum_half(1, ((y, ye), (x, xe)))
-        live = True
-        while live:
-            live = False
-            for half in halves:
-                try:
-                    next(half)
-                    live = True
-                except StopIteration:
-                    pass
-            if live:
-                yield
-
-        across_maps = []
-
-        def place(d, start, count):
-            return gfull.at[ch, 4 * k + (z + d) % 4, pl.ds(start, count)]
-
-        def also(d):
-            block = gfull.at[ch, 4 * k + (z + d) % 4]
-            across_maps.append(comm.send(block, block, sib))
-
-        yield from ring_gather(comm, place, ROWS, SPLIT, ze, also)
-        for copy in across_maps:
+            gs[ch, i, n : n + 16] = jnp.concatenate([maps, jnp.zeros((16, 128), BF)], axis=1)
+
+        moved = []
+        for off in (4, 3, 5, 2, 6, 1, 7):
+            i = (c + off) % 8
+            local_block(i)
+            moved.append(comm.send(gs.at[ch, i, whole], gd.at[ch, c, whole], {"section": i}))
+        local_block(c)
+        gd[ch, c, whole] = gs[ch, c, whole]
+        yield
+
+        def total_of(parts):
+            total = parts[0].astype(F32)
+            for part in parts[1:]:
+                total = total + part.astype(F32)
+            return total.astype(BF)
+
+        axes = ((x, lambda d: seq_of((x + d) % 4, y)), (y, lambda d: seq_of(x, (y + d) % 4)))
+
+        def spread_out(h, step, value):
+            mine, to = axes[h ^ step]
+            gx[ch, h, step, mine, whole] = value
+            block = gx.at[ch, h, step, mine, whole]
+            return [comm.send(block, block, to(d)) for d in (2, 1, 3)]
+
+        def gathered(h, step):
+            return total_of([gx[ch, h, step, at, whole] for at in range(4)])
+
+        for copy in moved:
             copy.wait_recv()
+        value = total_of([gd[ch, at, whole] for at in range(8)])
+        sent = [spread_out(h, 0, value[:, 128 * h : 128 * h + 128]) for h in range(2)]
+        yield
+        for h in range(2):
+            for copy in sent[h]:
+                copy.wait_recv()
+            sent[h] = spread_out(h, 1, gathered(h, 0))
+        yield
+        for h in range(2):
+            for copy in sent[h]:
+                copy.wait_recv()
+            gfull[ch, c, whole, 128 * h : 128 * h + 128] = gathered(h, 1)
+        block = gfull.at[ch, c, whole]
+        moved = [
+            comm.send(block, block, {"section": (c + off) % 8}) for off in (4, 3, 5, 2, 6, 1, 7)
+        ]
+        yield
+        for copy in moved:
+            copy.wait_recv()
+        yield
 
     lane8 = lax.broadcasted_iota(jnp.int32, (16, 1024), 1)
     row8 = lax.broadcasted_iota(jnp.int32, (16, 1024), 0)
@@ -503,19 +451,20 @@
         ]
 
     def prepare(ch):
+        first, count = CHUNKS[ch]
+        n = count // 8
         dtw = jnp.concatenate([dtw_ref[...], dtw_ref[...]], axis=0)
         dtb = twice(dtb_ref[...])
-        low = lax.broadcasted_iota(jnp.int32, (128, 128), 1) < 64
+        low = lax.broadcasted_iota(jnp.int32, (n, 128), 1) < 64
         for i in range(8):
-            rows = pl.ds(i * 128, 128)
-            pre = nt_dot(gfull[ch, i, 0:128], dtw) + dtb
+            rows = pl.ds(i * n, n)
+            pre = nt_dot(gfull[ch, i, 0:n], dtw) + dtb
             st = jnp.maximum(pre, 0.0) + jnp.log1p(jnp.exp(-jnp.abs(pre)))
             step_size[rows] = st
-            u = uz[pl.ds(ch * 1024 + i * 128, 128)].astype(BF).astype(F32)
+            u = uz[pl.ds(first + i * n, n)].astype(BF).astype(F32)
             drive[rows] = st * jnp.where(low, u, pltpu.roll(u, 64, 1))
-            wide[rows] = lax.dot_general(
-                gfull[ch, i, 128:ROWS, 0:128], spread, TN, preferred_element_type=F32
-            )
+            maps = gfull[ch, i, n : n + 16, 0:128]
+            wide[rows] = lax.dot_general(maps, spread, TN, preferred_element_type=F32)[0:n]
 
     nothing = jnp.zeros((8, 128), F32)
 
@@ -528,7 +477,7 @@
             for q in range(4)
         )
 
-    def segment_ends():
+    def segment_ends(ch):
         decay = decays()
 
         def first_pass(j, carried):
@@ -536,7 +485,9 @@
             st, states = advance(j, states, decay)
             return (total + st, states)
 
-        return lax.fori_loop(0, 128, first_pass, (nothing, (nothing,) * 4), unroll=8)
+        return lax.fori_loop(
+            0, CHUNKS[ch][1] // 8, first_pass, (nothing, (nothing,) * 4), unroll=8
+        )
 
     def entries(found, carry):
         total, ends = found
@@ -558,96 +509,99 @@
         return starts, after
 
     def finish(ch, starts):
+        first, count = CHUNKS[ch]
+        length = count // 8
         decay = decays()
         skip = twice(skip_ref[...])
 
         def second_pass(j, states):
             _, states = advance(j, states, decay)
             at = pl.ds(pl.multiple_of(j * 8, 8), 8)
-            gated = uz[pl.ds(pl.multiple_of(ch * 1024 + j * 8, 8), 8)]
+            gated = uz[pl.ds(pl.multiple_of(first + j * 8, 8), 8)]
             read = states[0] * wide[at, 512:640]
             for q in range(1, 4):
                 read = read + states[q] * wide[at, 512 + q * 128 : 640 + q * 128]
             read = read + pltpu.roll(read, 64, 1)
             u = gated.astype(BF).astype(F32)
-            ys[pl.ds(j, 8, stride=128), :] = (read + skip * u) * pltpu.roll(gated, 64, 1)
+            ys[pl.ds(j, 8, stride=length), :] = (read + skip * u) * pltpu.roll(gated, 64, 1)
             return states
 
-        lax.fori_loop(0, 128, second_pass, tuple(starts), unroll=8)
-        for seg in range(8):
-            block = jnp.transpose(ys[seg * 128 : (seg + 1) * 128, :])
-            column = ch * 1024 + seg * 128
-            out_ref[:, column : column + 128] = block[0:64].astype(BF)
-
-    pairs = {}
-
-    def go(pair, steps):
-        if pair not in pairs:
-            pairs[pair] = (unit(2 * pair), unit(2 * pair + 1))
-        for _ in range(steps):
-            for stream in pairs[pair]:
-                next(stream)
-
-    def advance_all(stream, steps=1):
-        for _ in range(steps):
-            next(stream, None)
-
-    run(act_steps)
-    for copy in across:
-        copy.wait_recv()
-
-    go(0, 3)
+        lax.fori_loop(0, length, second_pass, tuple(starts), unroll=8)
+        for at in range(0, count, 128):
+            block = jnp.transpose(ys[at : at + 128, :])
+            out_ref[:, first + at : first + at + 128] = block[0:64].astype(BF)
+
+    units = {}
+
+    def go(*steps):
+        for step in steps:
+            u, count = step // 10, step % 10
+            if u not in units:
+                units[u] = unit(u)
+            for _ in range(count):
+                next(units[u])
+
+    across[0].wait_recv()
+    go(1)
+    act_up.wait_recv()
+    far_up = pass_on(-1, ze[0], 0, 128)
+    across[-1] = pass_on(-1, sib)
+    act_down.wait_recv()
+    far_down = pass_on(1, ze[1], 128, 128)
+    across[1] = pass_on(1, sib)
+    go(1)
+    across[-1].wait_recv()
+    go(11, 1, 11)
+    far_up.wait_recv()
+    far_down.wait_recv()
+    across[2] = pass_on(2, sib)
+    go(11, 1)
+    across[1].wait_recv()
+    go(23)
     share_inverse()
-    go(0, 1)
-    go(1, 3)
-    go(0, 1)
-    go(1, 1)
-    go(0, 1)
-    go(2, 3)
+    go(11)
+    across[2].wait_recv()
+    go(33, 1, 11, 21, 31)
     for copy in inverses:
         copy.wait_recv()
-    go(0, 1)
-    go(1, 1)
-    go(2, 1)
-    go(1, 1)
-    go(3, 3)
-    go(1, 1)
+    go(43, 53, 1, 11, 1, 11, 21, 31, 41, 51, 21, 31, 63, 73, 21, 31)
     conv(0)
     maps0 = sum_maps(0)
-    advance_all(maps0)
-    go(2, 1)
-    advance_all(maps0)
-    go(3, 1)
-    advance_all(maps0)
-    go(2, 1)
-    advance_all(maps0)
-    go(3, 1)
-    advance_all(maps0)
-    go(2, 1)
-    advance_all(maps0)
-    go(3, 1)
-    advance_all(maps0)
-    go(3, 1)
-
+    next(maps0)
+    go(41, 51, 61, 71)
+    next(maps0)
+    go(41, 51, 41, 51)
     conv(1)
     maps1 = sum_maps(1)
-    advance_all(maps1)
-    advance_all(maps0)
-    advance_all(maps1)
-    for _ in maps0:
-        pass
+    next(maps1)
+    next(maps0)
+    go(61, 71)
+    next(maps1)
+    next(maps0)
+    go(61, 71)
+    next(maps1)
+    next(maps0)
+    go(61, 71)
+    conv(2)
+    maps2 = sum_maps(2)
+    next(maps2)
+    next(maps1)
     prepare(0)
-    advance_all(maps1)
-    found = segment_ends()
-    advance_all(maps1)
+    found = segment_ends(0)
+    next(maps2)
+    next(maps1)
     starts, carry = entries(found, None)
     finish(0, starts)
-    for _ in maps1:
-        pass
-
+    next(maps2)
     prepare(1)
-    starts, carry = entries(segment_ends(), carry)
+    found = segment_ends(1)
+    next(maps2)
+    starts, carry = entries(found, carry)
     finish(1, starts)
+    next(maps2)
+    prepare(2)
+    starts, carry = entries(segment_ends(2), carry)
+    finish(2, starts)
     comm.finish()
 
 
@@ -689,13 +643,10 @@
             pltpu.VMEM((8, 2, 256, 128), BF),
             pltpu.VMEM((2048, 128), F32),
             pltpu.VMEM((2048, 128), F32),
-            pltpu.VMEM((2, 8, ROWS, 256), BF),
-            pltpu.VMEM((2, 4, ROWS, 256), BF),
-            pltpu.VMEM((2, 3, 2, ROWS, 128), BF),
-            pltpu.VMEM((2, 2, 2, ROWS, 128), BF),
-            pltpu.VMEM((2, 2, ROWS, 128), BF),
-            pltpu.VMEM((2, 2, 2, 4, ROWS, 128), BF),
-            pltpu.VMEM((2, 8, ROWS, 256), BF),
+            pltpu.VMEM((3, 8, 144, 256), BF),
+            pltpu.VMEM((3, 8, 144, 256), BF),
+            pltpu.VMEM((3, 2, 2, 4, 144, 128), BF),
+            pltpu.VMEM((3, 8, 144, 256), BF),
             pltpu.VMEM((1024, 128), F32),
             pltpu.VMEM((1024, 1024), F32),
             pltpu.VMEM((1024, 128), F32),

time: 180 us -> 167 us (0.928)
  Pallas kernels: 178 us -> 165 us
    pallas_call x1, Pallas kernels: 178 us -> 165 us  [body(): pl.pallas_call(front_kernel, out_shape=jax.ShapeDtypeStruct((64, 2048), B...]
where the time goes in v3:
time: 167 us
  Pallas kernels  165 us (99%)
  local copies, waits for them, and re-layouts  1.67 us (1%)
    pallas_call x1, Pallas kernels, body(): pl.pallas_call(front_kernel, out_shape=jax.ShapeDtypeStruct((64, 2048), B...  165 us

profile of v3, /device:TPU:1, one launch (start us, length us, event | category | flops | bytes accessed | tf_op | source)
XLA Modules:
  0.0 166.5 jit_solution(17286836983880871581)
XLA Ops:
  0.0 164.8 %front.1 = bf16[64,2048]{1,0:T(8,128)(2,1)} custom-call(bf16[128,512]{1,0:T(8,128)(2,1)} %q_ref.1, bf16[128,128]{1,0:T(8,128)(2,1)} %k_ref.1, bf16[128,128]{1,0:T(8,128)(2,1)} %v_ref.1, bf16[2048,512]{1,0:T(8,128)(2,1)} %res_ref.1, bf16[512,512]{1,0:T(8,128)(2,1)} %ow_ref.1, f32[1,512]{1,0:T(1,128)} %bitcast.11, bf16[2,16,64,512]{3,2,1,0:T(8,128)(2,1)} %bitcast.8, ...), custom_call_target="tpu_custom_call" | custom-call | tf_op jit(solution)/shard_map/front/pallas_call | solution.py:615
  164.8 1.7 %copy.16 = bf16[64,2048]{1,0:T(8,128)(2,1)} copy(bf16[64,2048]{1,0:T(8,128)(2,1)} %front.1) | data formatting | bytes 524288

commit v4 on v3

--- a/solution.py
+++ b/solution.py
@@ -19,6 +19,7 @@
 F32 = jnp.float32
 CHUNKS = ((0, 1024), (1024, 512), (1536, 512))
 ORDER = (0, -1, 1, 2)
+SLOT = {0: 0, 1: 1, 3: 2}
 LOG2E = math.log2(math.e)
 NT = (((1,), (1,)), ((), ()))
 TN = (((0,), (0,)), ((), ()))
@@ -53,6 +54,7 @@
         return copy
 
     def finish(self):
+        assert len(self.copies) <= 480
         for copy in self.copies:
             copy.wait_send()
 
@@ -108,7 +110,7 @@
     q_ref, k_ref, v_ref, res_ref, ow_ref, gain_ref, w_ref, cw_ref, cb_ref, pw_ref,
     dtw_ref, dtb_ref, al_ref, skip_ref,
     out_ref,
-    kv, att, cs, cr, zs, zn, zf, act, hid, ssq_out, ssq_in, inv, res, wv,
+    kv, att, cs, cr, held, zs, zn, zf, act, ssq_out, ssq_in, inv, res, wv,
     s1, r1, s2, r2, own, t1, u1, t2, u2, mixed, uz,
     gs, gd, gx, gfull,
     step_size, wide, drive, ys,
@@ -131,11 +133,15 @@
     ze = (section_of((z + 1) % 4, k), section_of((z + 3) % 4, k))
     sib = section_of(z, o)
 
-    res_copy = pltpu.make_async_copy(
-        res_ref.at[pl.ds(1024 * k + 256 * z, 256)], res, local_sem.at[0]
-    )
-    res_copy.start()
-    w_copy = pltpu.make_async_copy(w_ref, wv, local_sem.at[1])
+    res_copies = [
+        pltpu.make_async_copy(
+            res_ref.at[pl.ds(1024 * ch + 256 * z + 128 * k, 128)], res.at[ch], local_sem.at[ch]
+        )
+        for ch in range(2)
+    ]
+    for copy in res_copies:
+        copy.start()
+    w_copy = pltpu.make_async_copy(w_ref, wv, local_sem.at[2])
     w_copy.start()
 
     barrier = pltpu.get_barrier_semaphore()
@@ -187,64 +193,86 @@
         gather_plane(comm, plane_place(att, False, 64), 64, ye, xe),
     )
 
-    def branch(kk, zt):
-        rows = att[2 * kk + zt // 2, pl.ds((zt % 2) * 2, 2)].reshape(256, 512)
+    w_copy.wait()
+    for copy in res_copies:
+        copy.wait()
+    across = ({}, {})
+    offsets = (2, 1, 3, 0)
+
+    def branch(ch, zt, kk):
+        rows = att[2 * ch + zt // 2, 2 * (zt % 2) + kk]
         return mm(rows, ow_ref[...])
 
-    offsets = (2, 1, 3, 0)
-    crossing = []
-    for off in offsets:
-        zt = (z + off) % 4
-        cs[zt] = branch(o, zt).astype(BF)
-        crossing.append(comm.send(cs.at[zt], cr.at[zt], sib))
-    w_copy.wait()
-    res_copy.wait()
-    near = []
-    for at, off in enumerate(offsets):
-        zt = (z + off) % 4
-        part = branch(k, zt)
-        crossing[at].wait_recv()
-        part = part + cr[zt].astype(F32)
-        if off == 2:
-            zs[0] = part.astype(BF)
-            far = (
-                comm.send(zs.at[0, 0:128], zf.at[0], ze[0]),
-                comm.send(zs.at[0, 128:256], zf.at[1], ze[1]),
-            )
-        elif off == 1:
-            far[0].wait_recv()
-            zs[1, 0:128] = (part[0:128] + zf[0].astype(F32)).astype(BF)
-            zs[1, 128:256] = part[128:256].astype(BF)
-            near.append(comm.send(zs.at[1], zn.at[0], ze[0]))
-        elif off == 3:
-            far[1].wait_recv()
-            zs[2, 0:128] = part[0:128].astype(BF)
-            zs[2, 128:256] = (part[128:256] + zf[1].astype(F32)).astype(BF)
-            near.append(comm.send(zs.at[2], zn.at[1], ze[1]))
-        else:
-            part = part + res[...].astype(F32)
-            near[0].wait_recv()
-            part = part + zn[0].astype(F32)
-            near[1].wait_recv()
-            hid[...] = part + zn[1].astype(F32)
-
-    hidden = hid[...]
-    act[k, z] = (hidden * gain_ref[...]).astype(BF)
-    def act_block(d, start=0, count=256):
-        return act.at[k, (z + d) % 4, pl.ds(start, count)]
-
-    def pass_on(d, dev, start=0, count=256):
-        block = act_block(d, start, count)
-        return comm.send(block, block, dev)
-
-    act_up, act_down = pass_on(0, ze[0]), pass_on(0, ze[1])
-    across = {0: pass_on(0, sib)}
-    ssq_out[...] = nt_dot(jnp.ones((8, 512), F32), hidden * hidden, precision=lax.Precision.HIGHEST)
-    ssq_in[s] = ssq_out[...]
-    squares = [
-        comm.send(ssq_out, ssq_in.at[s], {"seq": (s + off) % 16}) for off in range(1, 16)
-    ]
+    def section_sum(ch):
+        crossing = []
+        for off in offsets:
+            zt = (z + off) % 4
+            cs[ch, zt] = branch(ch, zt, o).astype(BF)
+            crossing.append(comm.send(cs.at[ch, zt], cr.at[ch, zt], sib))
+        yield
+        for at, off in enumerate(offsets):
+            zt = (z + off) % 4
+            part = branch(ch, zt, k)
+            crossing[at].wait_recv()
+            part = part + cr[ch, zt].astype(F32)
+            if off == 2:
+                zs[ch, 0] = part.astype(BF)
+                far = [
+                    comm.send(zs.at[ch, 0, 64 * e : 64 * e + 64], zf.at[ch, e], ze[e])
+                    for e in range(2)
+                ]
+            else:
+                held[ch, SLOT[off]] = part
+        yield
+        near = []
+        for e in range(2):
+            far[e].wait_recv()
+            rest = slice(64 - 64 * e, 128 - 64 * e)
+            same = slice(64 * e, 64 * e + 64)
+            slot = 1 if e == 0 else 2
+            source = 1 if e == 0 else 3
+            zs[ch, slot, rest] = sums(ch, source, rest).astype(BF)
+            zs[ch, slot, same] = (sums(ch, source, same) + zf[ch, e].astype(F32)).astype(BF)
+            near.append(comm.send(zs.at[ch, slot], zn.at[ch, e], ze[e]))
+        yield
+        part = sums(ch, 0, slice(0, 128)) + res[ch].astype(F32)
+        for e in range(2):
+            near[e].wait_recv()
+            part = part + zn[ch, e].astype(F32)
+        act[ch, z, k] = (part * gain_ref[...]).astype(BF)
+
+        def pass_on(d, dev, start=0, count=128):
+            block = act.at[ch, (z + d) % 4, k, pl.ds(start, count)]
+            return comm.send(block, block, dev)
+
+        up, down = pass_on(0, ze[0]), pass_on(0, ze[1])
+        across[ch][0] = pass_on(0, sib)
+        ssq_out[:, 128 * ch : 128 * ch + 128] = nt_dot(
+            jnp.ones((8, 512), F32), part * part, precision=lax.Precision.HIGHEST
+        )
+        yield
+        up.wait_recv()
+        far_up = pass_on(-1, ze[0], 0, 64)
+        across[ch][-1] = pass_on(-1, sib)
+        down.wait_recv()
+        far_down = pass_on(1, ze[1], 64, 64)
+        across[ch][1] = pass_on(1, sib)
+        yield
+        far_up.wait_recv()
+        far_down.wait_recv()
+        across[ch][2] = pass_on(2, sib)
+        yield
+
+    def sums(ch, off, rows):
+        return held[ch, SLOT[off], rows]
+
+    squares = []
     inverses = []
+
+    def share_squares():
+        ssq_in[s] = ssq_out[...]
+        for off in range(1, 16):
+            squares.append(comm.send(ssq_out, ssq_in.at[s], {"seq": (s + off) % 16}))
 
     def share_inverse():
         for copy in squares:
@@ -252,25 +280,25 @@
         total = ssq_in[0]
         for at in range(1, 16):
             total = total + ssq_in[at]
-        inv[k, z] = lax.rsqrt(total / D + NORM_EPS)
+        inv[z, k] = lax.rsqrt(total / D + NORM_EPS)
         for dz in range(4):
             for flip in range(2):
                 if dz or flip:
                     to = section_of((z + dz) % 4, (k + flip) % 2)
-                    inverses.append(comm.send(inv.at[k, z], inv.at[k, z], to))
-
-    def unit(u):
-        ch = u // 4
-        zt = u % 4 if ch else (z + ORDER[u]) % 4
-        by_y = u % 2 == 0
-        main, main_ends, side, side_ends = (y, ye, x, xe) if by_y else (x, xe, y, ye)
+                    inverses.append(comm.send(inv.at[z, k], inv.at[z, k], to))
+
+    def unit(pair, kk):
+        ch = pair // 4
+        u = 2 * pair + kk
+        zt = pair % 4 if ch else (z + ORDER[pair]) % 4
+        main, main_ends, side, side_ends = (x, xe, y, ye) if kk else (y, ye, x, xe)
 
         def product(p):
             rows = []
             for j in range(4):
-                b = (j * 4 + p) if by_y else (p * 4 + j)
+                b = (p * 4 + j) if kk else (j * 4 + p)
                 rows += [wv[0, b], wv[1, b]]
-            return nt_dot(act[ch, zt], jnp.concatenate(rows, axis=0))
+            return nt_dot(act[ch, zt, kk], jnp.concatenate(rows, axis=0))
 
         acc = product((main + 2) % 4)
         for j in range(4):
@@ -301,39 +329,35 @@
         for copy in (*early, *late):
             copy.wait_recv()
 
-        def summed(j):
-            return own[u, j] + r2[u, 0, j].astype(F32) + r2[u, 1, j].astype(F32)
-
-        def summed_rows(j, rest):
+        def summed(j, rows=slice(0, 128)):
             return (
-                own[u, j, rest] + r2[u, 0, j, rest].astype(F32) + r2[u, 1, j, rest].astype(F32)
+                own[u, j, rows] + r2[u, 0, j, rows].astype(F32) + r2[u, 1, j, rows].astype(F32)
             )
 
         t1[u] = summed((side + 2) % 4).astype(BF)
         last_far = [
-            comm.send(t1.at[u, 128 * e : 128 * e + 128], u1.at[u, e], side_ends[e])
+            comm.send(t1.at[u, 64 * e : 64 * e + 64], u1.at[u, e], side_ends[e])
             for e in range(2)
         ]
-        parts = summed((side + 1) % 4), summed((side + 3) % 4)
         last = []
         for e in range(2):
-            rest = slice(128 - 128 * e, 256 - 128 * e)
-            t2[u, e, rest] = parts[e][rest].astype(BF)
+            rest = slice(64 - 64 * e, 128 - 64 * e)
+            t2[u, e, rest] = summed((side + 1 + 2 * e) % 4, rest).astype(BF)
             last.append(comm.send(t2.at[u, e, rest], u2.at[u, e, rest], side_ends[e]))
         yield
         for e in range(2):
             last_far[e].wait_recv()
-            rest = slice(128 * e, 128 * e + 128)
-            j = (side + 1 + 2 * e) % 4
-            part = summed_rows(j, rest) + u1[u, e].astype(F32)
+            rest = slice(64 * e, 64 * e + 64)
+            part = summed((side + 1 + 2 * e) % 4, rest) + u1[u, e].astype(F32)
             t2[u, e, rest] = part.astype(BF)
             last.append(comm.send(t2.at[u, e, rest], u2.at[u, e, rest], side_ends[e]))
         yield
         for copy in last:
             copy.wait_recv()
         part = summed(side) + u2[u, 0].astype(F32) + u2[u, 1].astype(F32)
-        scale = jnp.transpose(inv[ch, zt])[:, 0:1]
-        mixed[pl.ds(pl.multiple_of(ch * 1024 + zt * 256, 256), 256)] = part * scale
+        scale = jnp.transpose(inv[zt, kk, :, 128 * ch : 128 * ch + 128])[:, 0:1]
+        at = pl.multiple_of(ch * 1024 + zt * 256 + kk * 128, 128)
+        mixed[pl.ds(at, 128)] = part * scale
         yield
 
     lane = lax.broadcasted_iota(jnp.int32, (8, 128), 1)
@@ -531,71 +555,74 @@
             block = jnp.transpose(ys[at : at + 128, :])
             out_ref[:, first + at : first + at + 128] = block[0:64].astype(BF)
 
-    units = {}
+    pairs = {}
 
     def go(*steps):
         for step in steps:
-            u, count = step // 10, step % 10
-            if u not in units:
-                units[u] = unit(u)
+            pair, count = step // 10, step % 10
+            if pair not in pairs:
+                pairs[pair] = (unit(pair, 0), unit(pair, 1))
             for _ in range(count):
-                next(units[u])
-
-    across[0].wait_recv()
-    go(1)
-    act_up.wait_recv()
-    far_up = pass_on(-1, ze[0], 0, 128)
-    across[-1] = pass_on(-1, sib)
-    act_down.wait_recv()
-    far_down = pass_on(1, ze[1], 128, 128)
-    across[1] = pass_on(1, sib)
-    go(1)
-    across[-1].wait_recv()
-    go(11, 1, 11)
-    far_up.wait_recv()
-    far_down.wait_recv()
-    across[2] = pass_on(2, sib)
+                for stream in pairs[pair]:
+                    next(stream)
+
+    sec0, sec1 = section_sum(0), section_sum(1)
+    for stream in (sec0, sec0, sec1, sec0, sec1, sec0, sec1):
+        next(stream)
+    across[0][0].wait_recv()
+    go(2)
+    next(sec0)
+    next(sec1)
+    share_squares()
+    across[0][-1].wait_recv()
+    go(11, 1, 12, 1)
+    next(sec0)
+    next(sec1)
+    across[0][1].wait_recv()
+    go(23, 11, 1)
+    across[0][2].wait_recv()
+    go(33, 21)
+    next(sec1)
     go(11, 1)
-    across[1].wait_recv()
-    go(23)
     share_inverse()
-    go(11)
-    across[2].wait_recv()
-    go(33, 1, 11, 21, 31)
+    for copy in across[1].values():
+        copy.wait_recv()
+    go(43, 31, 21, 11)
     for copy in inverses:
         copy.wait_recv()
-    go(43, 53, 1, 11, 1, 11, 21, 31, 41, 51, 21, 31, 63, 73, 21, 31)
+    go(53, 41, 31, 21, 1, 11)
+    go(63, 51, 41, 31, 21)
+    go(73, 61, 51, 41, 31)
     conv(0)
     maps0 = sum_maps(0)
     next(maps0)
-    go(41, 51, 61, 71)
+    go(71, 61, 51, 41)
     next(maps0)
-    go(41, 51, 41, 51)
+    go(71, 61, 51)
     conv(1)
     maps1 = sum_maps(1)
     next(maps1)
     next(maps0)
-    go(61, 71)
+    go(71, 61)
     next(maps1)
-    next(maps0)
-    go(61, 71)
-    next(maps1)
-    next(maps0)
-    go(61, 71)
+    go(71)
     conv(2)
     maps2 = sum_maps(2)
     next(maps2)
     next(maps1)
-    prepare(0)
-    found = segment_ends(0)
+    next(maps0)
     next(maps2)
     next(maps1)
+    next(maps0)
+    prepare(0)
+    next(maps2)
+    found = segment_ends(0)
+    next(maps1)
     starts, carry = entries(found, None)
+    next(maps2)
     finish(0, starts)
-    next(maps2)
     prepare(1)
     found = segment_ends(1)
-    next(maps2)
     starts, carry = entries(found, carry)
     finish(1, starts)
     next(maps2)
@@ -611,7 +638,7 @@
 ):
     vmem = pl.BlockSpec(memory_space=pltpu.VMEM)
     anyspace = pl.BlockSpec(memory_space=pl.ANY)
-    copies = 400
+    copies = 480
     return pl.pallas_call(
         front_kernel,
         out_shape=jax.ShapeDtypeStruct((64, 2048), BF),
@@ -620,27 +647,27 @@
         scratch_shapes=[
             pltpu.VMEM((4, 4, 128, 256), BF),
             pltpu.VMEM((4, 4, 128, 512), BF),
-            pltpu.VMEM((4, 256, 512), BF),
-            pltpu.VMEM((4, 256, 512), BF),
-            pltpu.VMEM((3, 256, 512), BF),
-            pltpu.VMEM((2, 256, 512), BF),
-            pltpu.VMEM((2, 128, 512), BF),
-            pltpu.VMEM((2, 4, 256, 512), BF),
-            pltpu.VMEM((256, 512), F32),
+            pltpu.VMEM((2, 4, 128, 512), BF),
+            pltpu.VMEM((2, 4, 128, 512), BF),
+            pltpu.VMEM((2, 3, 128, 512), F32),
+            pltpu.VMEM((2, 3, 128, 512), BF),
+            pltpu.VMEM((2, 2, 128, 512), BF),
+            pltpu.VMEM((2, 2, 64, 512), BF),
+            pltpu.VMEM((2, 4, 2, 128, 512), BF),
             pltpu.VMEM((8, 256), F32),
             pltpu.VMEM((16, 8, 256), F32),
-            pltpu.VMEM((2, 4, 8, 256), F32),
-            pltpu.VMEM((256, 512), BF),
+            pltpu.VMEM((4, 2, 8, 256), F32),
+            pltpu.VMEM((2, 128, 512), BF),
             pltpu.VMEM((2, 16, 64, 512), BF),
-            pltpu.VMEM((8, 4, 256, 128), BF),
-            pltpu.VMEM((8, 4, 256, 128), BF),
-            pltpu.VMEM((8, 2, 4, 256, 128), BF),
-            pltpu.VMEM((8, 2, 4, 256, 128), BF),
-            pltpu.VMEM((8, 4, 256, 128), F32),
-            pltpu.VMEM((8, 256, 128), BF),
-            pltpu.VMEM((8, 2, 128, 128), BF),
-            pltpu.VMEM((8, 2, 256, 128), BF),
-            pltpu.VMEM((8, 2, 256, 128), BF),
+            pltpu.VMEM((16, 4, 128, 128), BF),
+            pltpu.VMEM((16, 4, 128, 128), BF),
+            pltpu.VMEM((16, 2, 4, 128, 128), BF),
+            pltpu.VMEM((16, 2, 4, 128, 128), BF),
+            pltpu.VMEM((16, 4, 128, 128), F32),
+            pltpu.VMEM((16, 128, 128), BF),
+            pltpu.VMEM((16, 2, 64, 128), BF),
+            pltpu.VMEM((16, 2, 128, 128), BF),
+            pltpu.VMEM((16, 2, 128, 128), BF),
             pltpu.VMEM((2048, 128), F32),
             pltpu.VMEM((2048, 128), F32),
             pltpu.VMEM((3, 8, 144, 256), BF),
@@ -653,7 +680,7 @@
             pltpu.VMEM((1024, 128), F32),
             pltpu.SemaphoreType.DMA((copies,)),
             pltpu.SemaphoreType.DMA((copies,)),
-            pltpu.SemaphoreType.DMA((2,)),
+            pltpu.SemaphoreType.DMA((3,)),
         ],
         compiler_params=pltpu.CompilerParams(
             collective_id=0, has_side_effects=True, vmem_limit_bytes=60 * 1024 * 1024

time: 167 us -> 151 us (0.904)
  Pallas kernels: 165 us -> 150 us
    pallas_call x1, Pallas kernels: 165 us -> 150 us  [body(): pl.pallas_call(front_kernel, out_shape=jax.ShapeDtypeStruct((64, 2048), B...]
where the time goes in v4:
time: 151 us
  Pallas kernels  150 us (99%)
  local copies, waits for them, and re-layouts  1.67 us (1%)
    pallas_call x1, Pallas kernels, body(): pl.pallas_call(front_kernel, out_shape=jax.ShapeDtypeStruct((64, 2048), B...  150 us

profile of v4, /device:TPU:1, one launch (start us, length us, event | category | flops | bytes accessed | tf_op | source)
XLA Modules:
  0.0 151.3 jit_solution(4719774027505229524)
XLA Ops:
  0.0 149.6 %front.1 = bf16[64,2048]{1,0:T(8,128)(2,1)} custom-call(bf16[128,512]{1,0:T(8,128)(2,1)} %q_ref.1, bf16[128,128]{1,0:T(8,128)(2,1)} %k_ref.1, bf16[128,128]{1,0:T(8,128)(2,1)} %v_ref.1, bf16[2048,512]{1,0:T(8,128)(2,1)} %res_ref.1, bf16[512,512]{1,0:T(8,128)(2,1)} %ow_ref.1, f32[1,512]{1,0:T(1,128)} %bitcast.11, bf16[2,16,64,512]{3,2,1,0:T(8,128)(2,1)} %bitcast.8, ...), custom_call_target="tpu_custom_call" | custom-call | tf_op jit(solution)/shard_map/front/pallas_call | solution.py:642
  149.6 1.7 %copy.16 = bf16[64,2048]{1,0:T(8,128)(2,1)} copy(bf16[64,2048]{1,0:T(8,128)(2,1)} %front.1) | data formatting | bytes 524288

commit v5 on v4

--- a/solution.py
+++ b/solution.py
@@ -107,13 +107,14 @@
 
 
 def front_kernel(
-    q_ref, k_ref, v_ref, res_ref, ow_ref, gain_ref, w_ref, cw_ref, cb_ref, pw_ref,
+    q_hbm, k_ref, v_ref, res_ref, ow_hbm, gain_ref, w_ref, cw_ref, cb_ref, pw_ref,
     dtw_ref, dtb_ref, al_ref, skip_ref,
     out_ref,
     kv, att, cs, cr, held, zs, zn, zf, act, ssq_out, ssq_in, inv, res, wv,
     s1, r1, s2, r2, own, t1, u1, t2, u2, mixed, uz,
-    gs, gd, gx, gfull,
+    gs, gr, gz, gd, gx, gfull,
     step_size, wide, drive, ys,
+    q_ref, ow_ref,
     send_sem, recv_sem, local_sem,
 ):
     s = lax.axis_index("seq")
@@ -132,17 +133,6 @@
     ye = (seq_of(x, (y + 1) % 4), seq_of(x, (y + 3) % 4))
     ze = (section_of((z + 1) % 4, k), section_of((z + 3) % 4, k))
     sib = section_of(z, o)
-
-    res_copies = [
-        pltpu.make_async_copy(
-            res_ref.at[pl.ds(1024 * ch + 256 * z + 128 * k, 128)], res.at[ch], local_sem.at[ch]
-        )
-        for ch in range(2)
-    ]
-    for copy in res_copies:
-        copy.start()
-    w_copy = pltpu.make_async_copy(w_ref, wv, local_sem.at[2])
-    w_copy.start()
 
     barrier = pltpu.get_barrier_semaphore()
     for off in range(1, 16):
@@ -153,6 +143,21 @@
         pl.semaphore_signal(
             barrier, inc=1, device_id={"section": (c + off) % 8}, device_id_type=MESH
         )
+    res_copies = [
+        pltpu.make_async_copy(
+            res_ref.at[pl.ds(1024 * ch + 256 * z + 128 * k, 128)], res.at[ch], local_sem.at[ch]
+        )
+        for ch in range(2)
+    ]
+    for copy in res_copies:
+        copy.start()
+    q_copy = pltpu.make_async_copy(q_hbm, q_ref, local_sem.at[3])
+    q_copy.start()
+    ow_copy = pltpu.make_async_copy(ow_hbm, ow_ref, local_sem.at[4])
+    ow_copy.start()
+    w_copy = pltpu.make_async_copy(w_ref, wv, local_sem.at[2])
+    w_copy.start()
+
     kv[x, y, :, 0:HD] = k_ref[...]
     kv[x, y, :, HD:] = v_ref[...]
     pl.semaphore_wait(barrier, 22)
@@ -174,6 +179,8 @@
         gather_plane(comm, plane_place(kv, False, 64), 64, ye, xe),
     )
 
+    q_copy.wait()
+    ow_copy.wait()
     query_pos = s * 128 + lax.broadcasted_iota(jnp.int32, (128, 2048), 0)
     key_pos = lax.broadcasted_iota(jnp.int32, (128, 2048), 1)
     allowed = query_pos >= key_pos
@@ -413,13 +420,25 @@
             maps = nt_dot(map_weight, u).astype(BF)
             gs[ch, i, n : n + 16] = jnp.concatenate([maps, jnp.zeros((16, 128), BF)], axis=1)
 
+        crossing = {}
+        for off in offsets:
+            zt = (z + off) % 4
+            local_block(2 * zt + o)
+            crossing[off] = comm.send(gs.at[ch, 2 * zt + o, whole], gr.at[ch, zt, whole], sib)
+        for off in offsets:
+            local_block(2 * ((z + off) % 4) + k)
+        yield
         moved = []
-        for off in (4, 3, 5, 2, 6, 1, 7):
-            i = (c + off) % 8
-            local_block(i)
-            moved.append(comm.send(gs.at[ch, i, whole], gd.at[ch, c, whole], {"section": i}))
-        local_block(c)
-        gd[ch, c, whole] = gs[ch, c, whole]
+        for off in offsets:
+            zt = (z + off) % 4
+            crossing[off].wait_recv()
+            part = gs[ch, 2 * zt + k, whole].astype(F32) + gr[ch, zt, whole].astype(F32)
+            if off:
+                gz[ch, zt, whole] = part.astype(BF)
+                to = section_of(zt, k)
+                moved.append(comm.send(gz.at[ch, zt, whole], gd.at[ch, z, whole], to))
+            else:
+                gd[ch, z, whole] = part.astype(BF)
         yield
 
         def total_of(parts):
@@ -441,7 +460,7 @@
 
         for copy in moved:
             copy.wait_recv()
-        value = total_of([gd[ch, at, whole] for at in range(8)])
+        value = total_of([gd[ch, at, whole] for at in range(4)])
         sent = [spread_out(h, 0, value[:, 128 * h : 128 * h + 128]) for h in range(2)]
         yield
         for h in range(2):
@@ -454,11 +473,17 @@
                 copy.wait_recv()
             gfull[ch, c, whole, 128 * h : 128 * h + 128] = gathered(h, 1)
         block = gfull.at[ch, c, whole]
+        crossing = [comm.send(block, block, sib)]
         moved = [
-            comm.send(block, block, {"section": (c + off) % 8}) for off in (4, 3, 5, 2, 6, 1, 7)
+            comm.send(block, block, section_of((z + off) % 4, k)) for off in (2, 1, 3)
         ]
         yield
-        for copy in moved:
+        for at, off in ((1, 3), (2, 1), (0, 2)):
+            moved[at].wait_recv()
+            block = gfull.at[ch, 2 * ((z + off) % 4) + k, whole]
+            crossing.append(comm.send(block, block, sib))
+        yield
+        for copy in crossing:
             copy.wait_recv()
         yield
 
@@ -605,6 +630,7 @@
     next(maps0)
     go(71, 61)
     next(maps1)
+    next(maps0)
     go(71)
     conv(2)
     maps2 = sum_maps(2)
@@ -614,13 +640,18 @@
     next(maps2)
     next(maps1)
     next(maps0)
+    next(maps2)
+    next(maps1)
+    next(maps0)
     prepare(0)
     next(maps2)
+    next(maps1)
     found = segment_ends(0)
+    next(maps2)
     next(maps1)
     starts, carry = entries(found, None)
+    finish(0, starts)
     next(maps2)
-    finish(0, starts)
     prepare(1)
     found = segment_ends(1)
     starts, carry = entries(found, carry)
@@ -642,7 +673,7 @@
     return pl.pallas_call(
         front_kernel,
         out_shape=jax.ShapeDtypeStruct((64, 2048), BF),
-        in_specs=[vmem, vmem, vmem, anyspace, vmem, vmem, anyspace] + [vmem] * 7,
+        in_specs=[anyspace, vmem, vmem, anyspace, anyspace, vmem, anyspace] + [vmem] * 7,
         out_specs=vmem,
         scratch_shapes=[
             pltpu.VMEM((4, 4, 128, 256), BF),
@@ -671,16 +702,20 @@
             pltpu.VMEM((2048, 128), F32),
             pltpu.VMEM((2048, 128), F32),
             pltpu.VMEM((3, 8, 144, 256), BF),
-            pltpu.VMEM((3, 8, 144, 256), BF),
+            pltpu.VMEM((3, 4, 144, 256), BF),
+            pltpu.VMEM((3, 4, 144, 256), BF),
+            pltpu.VMEM((3, 4, 144, 256), BF),
             pltpu.VMEM((3, 2, 2, 4, 144, 128), BF),
             pltpu.VMEM((3, 8, 144, 256), BF),
             pltpu.VMEM((1024, 128), F32),
             pltpu.VMEM((1024, 1024), F32),
             pltpu.VMEM((1024, 128), F32),
             pltpu.VMEM((1024, 128), F32),
+            pltpu.VMEM((128, 512), BF),
+            pltpu.VMEM((512, 512), BF),
             pltpu.SemaphoreType.DMA((copies,)),
             pltpu.SemaphoreType.DMA((copies,)),
-            pltpu.SemaphoreType.DMA((3,)),
+            pltpu.SemaphoreType.DMA((5,)),
         ],
         compiler_params=pltpu.CompilerParams(
             collective_id=0, has_side_effects=True, vmem_limit_bytes=60 * 1024 * 1024

time: 151 us -> 150 us (level)
  Pallas kernels: 150 us -> 148 us
    pallas_call x1, Pallas kernels: 150 us -> 148 us  [body(): pl.pallas_call(front_kernel, out_shape=jax.ShapeDtypeStruct((64, 2048), B...]
where the time goes in v5:
time: 150 us; the launch traced here: 149 us
  Pallas kernels  148 us (99%)
  local copies, waits for them, and re-layouts  1.67 us (1%)
    pallas_call x1, Pallas kernels, body(): pl.pallas_call(front_kernel, out_shape=jax.ShapeDtypeStruct((64, 2048), B...  148 us

profile of v5, /device:TPU:1, one launch (start us, length us, event | category | flops | bytes accessed | tf_op | source)
XLA Modules:
  0.0 149.3 jit_solution(17785844595670504129)
XLA Ops:
  0.0 147.6 %front.1 = bf16[64,2048]{1,0:T(8,128)(2,1)} custom-call(bf16[128,512]{1,0:T(8,128)(2,1)} %q_hbm.1, bf16[128,128]{1,0:T(8,128)(2,1)} %k_ref.1, bf16[128,128]{1,0:T(8,128)(2,1)} %v_ref.1, bf16[2048,512]{1,0:T(8,128)(2,1)} %res_ref.1, bf16[512,512]{1,0:T(8,128)(2,1)} %ow_hbm.1, f32[1,512]{1,0:T(1,128)} %bitcast.11, bf16[2,16,64,512]{3,2,1,0:T(8,128)(2,1)} %bitcast.8, ...), custom_call_target="tpu_custom_call" | custom-call | tf_op jit(solution)/shard_map/front/pallas_call | solution.py:673
  147.6 1.7 %copy.16 = bf16[64,2048]{1,0:T(8,128)(2,1)} copy(bf16[64,2048]{1,0:T(8,128)(2,1)} %front.1) | data formatting | bytes 524288

commit v6 on v5

--- a/solution.py
+++ b/solution.py
@@ -111,7 +111,7 @@
     dtw_ref, dtb_ref, al_ref, skip_ref,
     out_ref,
     kv, att, cs, cr, held, zs, zn, zf, act, ssq_out, ssq_in, inv, res, wv,
-    s1, r1, s2, r2, own, t1, u1, t2, u2, mixed, uz,
+    s1, r1, s2, r2, own, t1, u1, t2, u2, t3, u3, mixed, uz,
     gs, gr, gz, gd, gx, gfull,
     step_size, wide, drive, ys,
     q_ref, ow_ref,
@@ -307,6 +307,11 @@
                 rows += [wv[0, b], wv[1, b]]
             return nt_dot(act[ch, zt, kk], jnp.concatenate(rows, axis=0))
 
+        def put_mixed(part):
+            scale = jnp.transpose(inv[zt, kk, :, 128 * ch : 128 * ch + 128])[:, 0:1]
+            at = pl.multiple_of(ch * 1024 + zt * 256 + kk * 128, 128)
+            mixed[pl.ds(at, 128)] = part * scale
+
         acc = product((main + 2) % 4)
         for j in range(4):
             s1[u, j] = acc[:, j * 128 : (j + 1) * 128].astype(BF)
@@ -341,6 +346,22 @@
                 own[u, j, rows] + r2[u, 0, j, rows].astype(F32) + r2[u, 1, j, rows].astype(F32)
             )
 
+        if pair >= 6:
+            direct = []
+            for d in (2, 1, 3):
+                t3[u - 12, d - 1] = summed((side + d) % 4).astype(BF)
+                to = seq_of(x, (y + d) % 4) if kk else seq_of((x + d) % 4, y)
+                direct.append(comm.send(t3.at[u - 12, d - 1], u3.at[u - 12, d - 1], to))
+            yield
+            yield
+            part = summed(side)
+            for copy in direct:
+                copy.wait_recv()
+            for d in range(3):
+                part = part + u3[u - 12, d].astype(F32)
+            put_mixed(part)
+            yield
+            return
         t1[u] = summed((side + 2) % 4).astype(BF)
         last_far = [
             comm.send(t1.at[u, 64 * e : 64 * e + 64], u1.at[u, e], side_ends[e])
@@ -362,9 +383,7 @@
         for copy in last:
             copy.wait_recv()
         part = summed(side) + u2[u, 0].astype(F32) + u2[u, 1].astype(F32)
-        scale = jnp.transpose(inv[zt, kk, :, 128 * ch : 128 * ch + 128])[:, 0:1]
-        at = pl.multiple_of(ch * 1024 + zt * 256 + kk * 128, 128)
-        mixed[pl.ds(at, 128)] = part * scale
+        put_mixed(part)
         yield
 
     lane = lax.broadcasted_iota(jnp.int32, (8, 128), 1)
@@ -592,7 +611,7 @@
                     next(stream)
 
     sec0, sec1 = section_sum(0), section_sum(1)
-    for stream in (sec0, sec0, sec1, sec0, sec1, sec0, sec1):
+    for stream in (sec0, sec1, sec0, sec1, sec0, sec1, sec0):
         next(stream)
     across[0][0].wait_recv()
     go(2)
@@ -628,12 +647,12 @@
     maps1 = sum_maps(1)
     next(maps1)
     next(maps0)
-    go(71, 61)
+    go(71, 61, 71)
+    conv(2)
+    maps2 = sum_maps(2)
+    next(maps2)
     next(maps1)
     next(maps0)
-    go(71)
-    conv(2)
-    maps2 = sum_maps(2)
     next(maps2)
     next(maps1)
     next(maps0)
@@ -651,7 +670,6 @@
     next(maps1)
     starts, carry = entries(found, None)
     finish(0, starts)
-    next(maps2)
     prepare(1)
     found = segment_ends(1)
     starts, carry = entries(found, carry)
@@ -699,6 +717,8 @@
             pltpu.VMEM((16, 2, 64, 128), BF),
             pltpu.VMEM((16, 2, 128, 128), BF),
             pltpu.VMEM((16, 2, 128, 128), BF),
+            pltpu.VMEM((4, 3, 128, 128), BF),
+            pltpu.VMEM((4, 3, 128, 128), BF),
             pltpu.VMEM((2048, 128), F32),
             pltpu.VMEM((2048, 128), F32),
             pltpu.VMEM((3, 8, 144, 256), BF),

time: 150 us -> 144 us (0.960)
  Pallas kernels: 148 us -> 143 us
    pallas_call x1, Pallas kernels: 148 us -> 143 us  [body(): pl.pallas_call(front_kernel, out_shape=jax.ShapeDtypeStruct((64, 2048), B...]
where the time goes in v6:
time: 144 us
  Pallas kernels  143 us (99%)
  local copies, waits for them, and re-layouts  1.67 us (1%)
    pallas_call x1, Pallas kernels, body(): pl.pallas_call(front_kernel, out_shape=jax.ShapeDtypeStruct((64, 2048), B...  143 us

profile of v6, /device:TPU:1, one launch (start us, length us, event | category | flops | bytes accessed | tf_op | source)
XLA Modules:
  0.0 144.3 jit_solution(5975035068342417936)
XLA Ops:
  0.0 142.6 %front.1 = bf16[64,2048]{1,0:T(8,128)(2,1)} custom-call(bf16[128,512]{1,0:T(8,128)(2,1)} %q_hbm.1, bf16[128,128]{1,0:T(8,128)(2,1)} %k_ref.1, bf16[128,128]{1,0:T(8,128)(2,1)} %v_ref.1, bf16[2048,512]{1,0:T(8,128)(2,1)} %res_ref.1, bf16[512,512]{1,0:T(8,128)(2,1)} %ow_hbm.1, f32[1,512]{1,0:T(1,128)} %bitcast.11, bf16[2,16,64,512]{3,2,1,0:T(8,128)(2,1)} %bitcast.8, ...), custom_call_target="tpu_custom_call" | custom-call | tf_op jit(solution)/shard_map/front/pallas_call | solution.py:691
  142.6 1.7 %copy.16 = bf16[64,2048]{1,0:T(8,128)(2,1)} copy(bf16[64,2048]{1,0:T(8,128)(2,1)} %front.1) | data formatting | bytes 524288

commit v7 on v6

--- a/solution.py
+++ b/solution.py
@@ -78,6 +78,7 @@
         block = place(df, 0, 0, size)
         return comm.send(block, block, second[0]), comm.send(block, block, second[1])
 
+    yield
     sent = [(0, along(0))]
     yield
     one.wait_recv()
@@ -86,6 +87,7 @@
     two.wait_recv()
     block = place(1, 0, half, size - half)
     four = comm.send(block, block, first[1])
+    yield
     sent.append((-1, along(-1)))
     sent.append((1, along(1)))
     yield

time: 144 us -> 143 us (level)
  Pallas kernels: 143 us -> 141 us
where the time goes in v7:
time: 143 us
  Pallas kernels  141 us (99%)
  local copies, waits for them, and re-layouts  1.67 us (1%)
    pallas_call x1, Pallas kernels, body(): pl.pallas_call(front_kernel, out_shape=jax.ShapeDtypeStruct((64, 2048), B...  141 us

profile of v7, /device:TPU:1, one launch (start us, length us, event | category | flops | bytes accessed | tf_op | source)
XLA Modules:
  0.0 143.1 jit_solution(3751790684040776938)
XLA Ops:
  0.0 141.4 %front.1 = bf16[64,2048]{1,0:T(8,128)(2,1)} custom-call(bf16[128,512]{1,0:T(8,128)(2,1)} %q_hbm.1, bf16[128,128]{1,0:T(8,128)(2,1)} %k_ref.1, bf16[128,128]{1,0:T(8,128)(2,1)} %v_ref.1, bf16[2048,512]{1,0:T(8,128)(2,1)} %res_ref.1, bf16[512,512]{1,0:T(8,128)(2,1)} %ow_hbm.1, f32[1,512]{1,0:T(1,128)} %bitcast.11, bf16[2,16,64,512]{3,2,1,0:T(8,128)(2,1)} %bitcast.8, ...), custom_call_target="tpu_custom_call" | custom-call | tf_op jit(solution)/shard_map/front/pallas_call | solution.py:693
  141.4 1.7 %copy.16 = bf16[64,2048]{1,0:T(8,128)(2,1)} copy(bf16[64,2048]{1,0:T(8,128)(2,1)} %front.1) | data formatting | bytes 524288
